TPU v7x, 128 devices: a whole 4x4x4 slice. The times are simulated.
128 devices in a mesh: row: 16 (over z_lo, x, core), col: 8 (over z_hi, y).
Axes of the slice: x: 4, y: 4, z: 4 (z_hi: 2, z_lo: 2; z = z_hi * 2 + z_lo), core: 2. Of those that a mesh axis runs over, the one named last changes fastest.
Arguments:
- inverse_front: float32 [16384, 16384], P('row', 'col'), may hold values from -0.09375 to 0.09375
- factor: float32 [4096, 1024], P('row'), may hold values from -1.2 to 1.2
- unit_lower: float32 [2, 512, 512], replicated, may hold values from -0.25 to 0.25
- pivot_inverse: float32 [2, 512], replicated, may hold values from 0.5 to 4
- tile_list: int32 [2, 16], replicated, may hold values from 0 to 63, as said below
- tile_valid: int32 [2, 16], replicated, may hold values from 0 to 1, as said below
Outputs:
- inverse_column: float32 [16384, 1024], P('row')
- diagonal_block: float32 [2, 512, 512], replicated
Inputs may be any that keep to these rules, and one draw needn't show every extreme that they name: `tile_list`: each row names 16 different tile rows of the front in increasing order, exactly 1 of them among each aligned group of 4 tile rows, and the last tile row is always among them. `tile_valid`: each row holds at least one 1.
All inputs are finite; a program needn't handle non-finite values.
Results may differ from a plain program's by a relative error of at most 0.0001.
Values sent between devices are 32-bit elements; how exact they have to be, the bound alone decides.
A program may use at most 192 MiB of HBM per device.

v0:
```python
import jax
import jax.numpy as jnp
from jax import lax
from jax.sharding import PartitionSpec as P

B = 256
W = 512
NS = 2
NA = 16


def from_root(block, axis, owner):
    block = jnp.where(lax.axis_index(axis) == owner, block, jnp.zeros_like(block))
    return lax.psum(block, axis)


def inner_left(left, right):
    return lax.dot_general(
        left,
        right,
        (((0,), (0,)), ((), ())),
        precision=lax.Precision.HIGHEST,
        preferred_element_type=jnp.float32,
    )


def shards(inverse_front, factor, unit_lower, pivot_inverse, tile_list, tile_valid):
    row_count = lax.axis_size("row")
    col_count = lax.axis_size("col")
    row_span, col_span = inverse_front.shape
    row_index = lax.axis_index("row")
    col_index = lax.axis_index("col")
    identity = jnp.eye(W, dtype=jnp.float32)
    inverses = [jnp.tril(unit_lower[member], -1) + identity for member in range(NS)]

    def normalize(slab):
        return jnp.concatenate(
            [
                jnp.dot(
                    slab[:, member * W : (member + 1) * W],
                    inverses[member],
                    precision=lax.Precision.HIGHEST,
                    preferred_element_type=jnp.float32,
                )
                for member in range(NS)
            ],
            axis=1,
        )

    normalized = lax.all_gather(normalize(factor), "row", axis=0, tiled=True)
    slot_tiles = normalized.reshape(NA, B, NS, W)

    def place_tiles(first, number):
        global_tile = first + jnp.arange(number, dtype=jnp.int32)
        onehot = (
            (tile_list[:, None, :] == global_tile[None, :, None]) & (tile_valid[:, None, :] > 0)
        ).astype(jnp.float32)
        placed = jnp.einsum("sta,absw->tbsw", onehot, slot_tiles, precision=lax.Precision.HIGHEST)
        return (placed.reshape(number * B, NS * W), jnp.sum(onehot, axis=2))

    row_factor, row_chosen = place_tiles(row_index * (row_span // B), row_span // B)
    col_factor, col_chosen = place_tiles(col_index * (col_span // B), col_span // B)
    row_global = row_index * row_span + jnp.arange(row_span, dtype=jnp.int32)
    col_global = col_index * col_span + jnp.arange(col_span, dtype=jnp.int32)
    lower_part = jnp.where(row_global[:, None] >= col_global[None, :], inverse_front, 0.0)
    lower_prod = jnp.dot(
        lower_part, col_factor, precision=lax.Precision.HIGHEST, preferred_element_type=jnp.float32
    )
    strict = jnp.where(row_global[:, None] > col_global[None, :], inverse_front, 0.0)
    mirror_prod = inner_left(strict, row_factor)
    row_total = lax.psum(lower_prod, "col")
    col_total = lax.psum(mirror_prod, "row")
    grid_ratio = row_count // col_count
    offset = row_index % grid_ratio * row_span
    own_piece = lax.dynamic_slice_in_dim(col_total, offset, row_span, 0)
    mirrored = from_root(own_piece, "col", row_index // grid_ratio)
    keep_rows = jnp.repeat(row_chosen, B, axis=1)
    keep_mask = jnp.repeat(keep_rows.T, W, axis=1)
    column = -(row_total + mirrored) * keep_mask
    base_block = jnp.stack(
        [
            jnp.dot(
                inverses[member].T * pivot_inverse[member][None, :],
                inverses[member],
                precision=lax.Precision.HIGHEST,
                preferred_element_type=jnp.float32,
            )
            for member in range(NS)
        ]
    )
    diag_terms = jnp.stack(
        [
            inner_left(
                row_factor[:, member * W : (member + 1) * W],
                column[:, member * W : (member + 1) * W],
            )
            for member in range(NS)
        ]
    )
    diag_total = lax.psum(diag_terms, "row")
    diagonal_block = base_block - diag_total
    return (column, diagonal_block)


def solution(mesh):
    in_specs = (P("row", "col"), P("row", None), P(), P(), P(), P())
    out_specs = (P("row", None), P())
    return jax.shard_map(shards, mesh=mesh, in_specs=in_specs, out_specs=out_specs, check_vma=False)
```

profile of v0, /device:TPU:1, one launch (start us, length us, event | category | flops | bytes accessed | tf_op | source)
XLA Modules:
  0.0 620.7 jit_solution(13033368712311143179)
XLA Ops:
  7.2 3.3 convolution_bitcast_fusion.1
  10.5 3.3 convolution_bitcast_fusion.2
  13.8 1.0 pad_maximum_fusion.1
  15.0 95.2 %all-gather.2.cloned.1.call-done = f32[4096,1024]{0,1:T(8,128)} async-done(((f32[256,1024]{0,1:T(8,128)}), f32[4096,1024]{0,1:T(8,128)}) %all-gather.2.cloned.1.call-update) | async-done | bytes 16777232 | tf_op jit(solution)/shard_map/all_gather | solution.py:50
  110.2 11.0 %copy.23 = f32[128,8,16,256]{3,2,1,0:T(8,128)S(1)} copy(f32[128,8,16,256]{3,1,2,0:T(8,128)} %bitcast.71) | data formatting | bytes 33554432
  121.2 6.5 %fusion.57 = f32[2,256,512,4]{1,3,2,0:T(4,128)S(1)} fusion(f32[16,256,2,512]{1,0,3,2:T(8,128)S(1)} %bitcast.67, s32[2,16]{1,0:T(2,128)S(1)} %copy-done.5, pred[2,16]{1,0:T(4,128)(4,1)S(1)} %broadcast_compare_fusion, s32[4]{0:T(128)S(1)} %iota_add_fusion.3), kind=kOutput, calls=%fused_computation.60 | convolution fusion | flops 201326848 | bytes 20971696 | tf_op jit(solution)/shard_map/sta,absw->tbsw/dot_general | solution.py:58
  127.7 1.0 copy.25
  128.8 2.0 copy-done.2
  130.8 57.2 %fusion = f32[2048,1024]{1,0:T(8,128)} fusion(f32[1024,1024]{0,1:T(8,128)S(1)} %bitcast.72, f32[1024,2048]{1,0:T(8,128)} %param.6, s32[2048]{0:T(1024)S(1)} %iota_add_fusion, s32[1024]{0:T(1024)S(1)} %iota_add_fusion.1), kind=kOutput, calls=%fused_computation | convolution fusion | flops 25773998080 | bytes 20983808 | tf_op jit(solution)/shard_map/dot_general | solution.py:18
  188.0 0.0 all-reduce.8.cloned.1.call-start
  188.1 20.3 %copy.14 = f32[16,256,2,512]{3,0,1,2:T(8,128)} copy(f32[16,256,2,512]{1,0,3,2:T(8,128)} %bitcast.68) | data formatting | bytes 33554432 | tf_op jit(solution)/shard_map/reshape | solution.py:51
  208.4 11.9 %convolution_bitcast_fusion = f32[8,256,2,512]{3,0,1,2:T(8,128)} fusion(f32[16,256,2,512]{3,0,1,2:T(8,128)} %copy.14, s32[2,16]{1,0:T(2,128)S(1)} %copy-done.5, s32[8]{0:T(128)S(1)} %iota_add_fusion.4, pred[2,16]{1,0:T(4,128)(4,1)S(1)} %broadcast_compare_fusion), kind=kOutput, calls=%fused_computation.14 | convolution fusion | flops 402653696 | bytes 25166016 | tf_op jit(solution)/shard_map/sta,absw->tbsw/dot_general | solution.py:58
  220.4 10.5 %copy.15 = f32[8,256,2,512]{1,0,3,2:T(8,128)} copy(f32[8,256,2,512]{3,0,1,2:T(8,128)} %convolution_bitcast_fusion) | data formatting | bytes 16777216 | tf_op jit(solution)/shard_map/sta,absw->tbsw/transpose | solution.py:58
  230.8 10.9 %copy.24 = f32[128,8,8,256]{3,1,2,0:T(8,128)} copy(f32[128,8,8,256]{3,2,1,0:T(8,128)} %bitcast.69) | data formatting | bytes 16777216
  241.8 87.7 %all-reduce.4.cloned.1.call-done = f32[2048,1024]{1,0:T(8,128)} async-done(((f32[2048,1024]{1,0:T(8,128)}), f32[2048,1024]{1,0:T(8,128)}) %all-reduce.4.cloned.1.call-update) | async-done | bytes 8388624 | tf_op jit(solution)/shard_map/psum | solution.py:72
  329.5 33.9 %select_add_fusion = f32[1024,1024]{1,0:T(8,128)} fusion(f32[2048,1024]{1,0:T(8,128)} %all-reduce.4.cloned.1.call-done, s32[]{:T(128)S(6)} %select_n.43, pred[]{:T(512)S(6)} %eq.40, f32[2048,1024]{0,1:T(8,128)} %bitcast.77, f32[1024,2048]{1,0:T(8,128)} %param.6, s32[2048]{0:T(1024)S(1)} %iota_add_fusion, s32[1024]{0:T(1024)S(1)} %iota_add_fusion.1), kind=kOutput, calls=%fused_computation.7 | convolution fusion | flops 25776095232 | bytes 25178116 | tf_op jit(solution)/shard_map/dot_general | solution.py:66
  363.4 0.2 all-reduce.6.cloned.1.call-start
  363.6 0.2 convert_reduce_fusion
  363.8 0.1 copy.17
  363.9 1.4 broadcast_in_dim.33
  365.3 3.0 copy.26
  368.3 106.8 %all-reduce.8.cloned.1.call-done = f32[1024,1024]{1,0:T(8,128)} async-done(((f32[1024,1024]{1,0:T(8,128)}), f32[1024,1024]{1,0:T(8,128)}) %all-reduce.8.cloned.1.call-update) | async-done | bytes 4194320 | tf_op jit(solution)/shard_map/psum | solution.py:71
  475.1 4.6 negate_multiply_fusion
  479.7 0.1 copy-done.3
  479.8 3.5 fusion.35
  483.3 3.5 fusion.30
  486.8 1.5 pad_maximum_fusion
  488.4 0.8 copy-done.4
  489.2 2.3 fusion.27
  491.5 3.3 fusion.24
  494.8 115.6 %all-reduce.6.cloned.1.call-done = f32[2,512,512]{2,1,0:T(8,128)} async-done(((f32[2,512,512]{2,1,0:T(8,128)}), f32[2,512,512]{2,1,0:T(8,128)}) %all-reduce.6.cloned.1.call-update) | async-done | bytes 2097168 | tf_op jit(solution)/shard_map/psum | solution.py:100
  610.4 3.7 maximum_subtract_fusion
  (27 shorter events, 0.3 us)
Async XLA Ops:
  7.2 7.8 %copy-start.7 = (s32[2,16]{1,0:T(2,128)S(1)}, s32[2,16]{1,0:T(2,128)}, u32[]{:S(2)}) copy-start(s32[2,16]{1,0:T(2,128)} %param.11) | copy-start | bytes 388
  7.2 103.1 %all-gather.2.cloned.1.call-start = ((), (), s32[]{:S(2)}) async-start(), calls=%async_computation | async-start | bytes 17825792 | tf_op jit(solution)/shard_map/all_gather | solution.py:50
  14.9 314.6 %all-reduce.4.cloned.1.call-start = ((), (), s32[]{:S(2)}) async-start(), calls=%async_computation.1 | async-start | bytes 16777216 | tf_op jit(solution)/shard_map/psum | solution.py:72
  110.2 11.0 %copy-start.5 = (s32[2,16]{1,0:T(2,128)S(1)}, s32[2,16]{1,0:T(2,128)}, u32[]{:S(2)}) copy-start(s32[2,16]{1,0:T(2,128)} %param.10) | copy-start | bytes 388
  121.2 6.5 %copy-start = (f32[128,8,16,256]{3,2,1,0:T(8,128)}, f32[128,8,16,256]{3,2,1,0:T(8,128)S(1)}, u32[]{:S(2)}) copy-start(f32[128,8,16,256]{3,2,1,0:T(8,128)S(1)} %copy.23) | copy-start | bytes 50331652
  128.8 2.1 copy-start.2
  188.0 287.1 %all-reduce.8.cloned.1.call-start = ((), (), s32[]{:S(2)}) async-start(), calls=%async_computation.3 | async-start | bytes 8388608 | tf_op jit(solution)/shard_map/psum | solution.py:71
  363.4 247.0 %all-reduce.6.cloned.1.call-start = ((), (), s32[]{:S(2)}) async-start(), calls=%async_computation.2 | async-start | bytes 4194304 | tf_op jit(solution)/shard_map/psum | solution.py:100
  475.1 4.6 copy-start.3
  479.8 7.0 %copy-start.1 = (f32[1024,1024]{1,0:T(8,128)}, f32[1024,1024]{1,0:T(8,128)S(1)}, u32[]{:S(2)}) copy-start(f32[1024,1024]{1,0:T(8,128)S(1)} %negate_multiply_fusion) | copy-start | bytes 12582916
  486.8 1.5 copy-start.6
  486.8 2.4 copy-start.4
Sparse Core Ops, SparseCore 0:
  15.0 95.2 all-gather.1
  188.1 141.3 all-reduce.3
  363.5 111.5 all-reduce.7
  488.5 121.8 all-reduce.5
where the time goes:
time: 629 us; the launch traced here: 621 us
  waiting for transfers between devices  405 us (64%)
  matrix products  129 us (21%)
  local copies, waits for them, and re-layouts  61.2 us (10%)
  between operations  14.2 us (2%)
  other arithmetic  10.9 us (2%)
    psum x1, waiting for transfers between devices, shards(): diag_total = lax.psum(diag_terms, 'row')  116 us
    psum x1, waiting for transfers between devices, shards(): row_total = lax.psum(lower_prod, 'col')  107 us
    all_gather x1, waiting for transfers between devices, shards(): normalized = lax.all_gather(normalize(factor), 'row', axis=0, tiled=True)  95.2 us
    psum x1, waiting for transfers between devices, shards(): col_total = lax.psum(mirror_prod, 'row')  87.7 us
    dot_general x3, matrix products, inner_left(): lax.dot_general(left, right, (((0,), (0,)), ((), ())), precision=lax.Prec...  64.2 us
    dot_general x1, matrix products, shards(): jnp.dot(lower_part, col_factor, precision=lax.Precision.HIGHEST, preferre...  33.9 us
    unnamed x20, local copies, waits for them, and re-layouts  28.9 us
    reshape x1, local copies, waits for them, and re-layouts, shards(): slot_tiles = normalized.reshape(NA, B, NS, W)  20.3 us
  transfers between devices with their start and end apart: 4, of which 4 were waited for; matrix products, arithmetic and copies ran while one was open for 10% of the time, Pallas kernels for 0%

commit v1 on v0

v1 whole, which is shorter than its diff:
```python
import jax
import jax.numpy as jnp
from jax import lax
from jax.experimental import pallas as pl
from jax.experimental.pallas import tpu as pltpu
from jax.sharding import PartitionSpec as P

B = 256
W = 512
NS = 2
NA = 16
NC = 8
LANES = 128
PIECE = W // NA
MESH = pl.DeviceIdType.MESH
F32 = jnp.float32
BF16 = jnp.bfloat16


def split(x):
    hi = x.astype(BF16)
    return hi, (x - hi.astype(F32)).astype(BF16)


def mm(a, b, dims=(1, 0)):
    def dot(x, y):
        return lax.dot_general(x, y, (((dims[0],), (dims[1],)), ((), ())), preferred_element_type=F32)

    return dot(a[0], b[0]) + (dot(a[0], b[1]) + dot(a[1], b[0]))


def prepare(tile_list, tile_valid, front, factor, lower, pivot, tiles_out, norm_out, base_out, sems):
    r = lax.axis_index("row")
    c = lax.axis_index("col")
    copies = []
    for s in range(NS):
        for j in range(2):
            row = (tile_list[s, r] - 4 * r) * B
            col = (tile_list[s, 2 * c + j] - 8 * c) * B
            src = front.at[pl.ds(pl.multiple_of(row, B), B), pl.ds(pl.multiple_of(col, B), B)]
            copies.append(pltpu.make_async_copy(src, tiles_out.at[2 * s + j], sems.at[2 * s + j]))
    for copy in copies:
        copy.start()
    i0 = lax.broadcasted_iota(jnp.int32, (W, W), 0)
    i1 = lax.broadcasted_iota(jnp.int32, (W, W), 1)
    for s in range(NS):
        inv = jnp.where(i0 > i1, lower[s], jnp.where(i0 == i1, 1.0, 0.0))
        keep = (tile_valid[s, r] > 0).astype(F32)
        fac = factor[:, s * W : (s + 1) * W] * keep
        inv_split = split(inv)
        norm_out[s] = mm(split(fac), inv_split)

        @pl.when(c // 4 == s)
        def _():
            i2 = lax.broadcasted_iota(jnp.int32, (W, LANES), 0)
            i3 = lax.broadcasted_iota(jnp.int32, (W, LANES), 1) + (c % 4) * LANES
            lanes = pl.ds(pl.multiple_of((c % 4) * LANES, LANES), LANES)
            part = jnp.where(i2 > i3, lower[s, :, lanes], jnp.where(i2 == i3, 1.0, 0.0))
            scaled = part * pivot[s].T
            base_out[...] = mm(inv_split, split(scaled), (0, 0))

    for copy in copies:
        copy.wait()
    own = r - 2 * c
    b0 = lax.broadcasted_iota(jnp.int32, (B, B), 0)
    b1 = lax.broadcasted_iota(jnp.int32, (B, B), 1)
    for j in range(2):

        @pl.when(own == j)
        def _():
            for s in range(NS):
                tile = tiles_out[2 * s + j]
                tiles_out[2 * s + j] = jnp.where(b0 >= b1, tile, tile.T)


def exchange(
    tiles, norm, base, c_all, d_all,
    st, nr, q_loc, q_rx, p_out, q_out, c_rx, d_part, d_rx,
    st_s, st_r, n_s, n_r, g_s, g_r, q_s, q_r, p_ss, q_ss, c_r, ca_s, ca_r, dp_s, dp_r, da_s, da_r, db_s, db_r, dc_s, dc_r,
):
    r = lax.axis_index("row")
    c = lax.axis_index("col")
    k = r // 2
    q = r % 2
    cy = c % 4
    cz = c // 4
    sib = (r + 1 - 2 * q, c)
    lower = k > c
    upper = k < c
    off = k != c
    diag = k == c
    s_own = jnp.where(lower, 0, 1)
    pending = []

    def copy(src, dst, ssem, rsem, dev):
        return pltpu.make_async_remote_copy(
            src_ref=src, dst_ref=dst, send_sem=ssem, recv_sem=rsem, device_id=dev, device_id_type=MESH
        )

    def send(cond, make):
        pl.when(cond)(lambda: make().start())
        pending.append((cond, make))

    def arrived(buf, sem):
        copy(buf, buf, sem, sem, sib).wait_recv()

    for j in range(2):
        send(lower, lambda j=j: copy(tiles.at[2 + j], st.at[q], st_s.at[j], st_r.at[q], (2 * c + j, k)))
    send(off, lambda: copy(norm.at[1 - s_own], nr.at[q], n_s.at[0], n_r.at[q], (2 * c + q, k)))
    send(diag & (q == 0), lambda: copy(norm, nr, g_s.at[0], g_r.at[2], sib))

    def ship(slices, sems, s, row, slot):
        for d in range(4):
            def make(d=d):
                return copy(slices.at[d], c_rx.at[slot], sems.at[d], c_r.at[slot], (row, 4 * s + d))
            yield d, make

    def send_slices(cond, slices, sems, s, row, slot):
        for d, make in ship(slices, sems, s, row, slot):
            mine = (row == r) & (4 * s + d == c)
            send(cond & jnp.logical_not(mine), make)

            @pl.when(cond & mine)
            def _():
                c_rx[slot] = slices[d]

    n_own = norm.at[s_own]

    @pl.when(off)
    def _():
        own = split(n_own[...])
        for j in range(2):

            @pl.when(lower)
            def _():
                q_loc[j] = mm(split(tiles[j]), own, (0, 0))

            @pl.when(upper)
            def _():
                arrived(st.at[j], st_r.at[j])
                q_loc[j] = mm(split(st[j]), own)

    send(off, lambda: copy(q_loc.at[1 - q], q_rx.at[0], q_s.at[0], q_r.at[0], sib))

    @pl.when(off)
    def _():
        arrived(nr.at[q], n_r.at[q])

    send(off, lambda: copy(nr.at[q], nr.at[q], g_s.at[1], g_r.at[q], sib))

    @pl.when(off)
    def _():
        arrived(q_rx.at[0], q_r.at[0])
        for d in range(4):
            lanes = slice(d * LANES, (d + 1) * LANES)
            q_out[d] = q_loc[q, :, lanes] + q_rx[0, :, lanes]

    send_slices(off, q_out, q_ss, s_own, 2 * c + q, k)

    @pl.when(off)
    def _():
        arrived(nr.at[1 - q], g_r.at[1 - q])

        def put(value):
            for d in range(4):
                p_out[0, d] = value[:, d * LANES : (d + 1) * LANES]

        @pl.when(lower)
        def _():
            put(mm(split(tiles[0]), split(nr[0])) + mm(split(tiles[1]), split(nr[1])))

        @pl.when(upper)
        def _():
            put(mm(split(st[0]), split(nr[0]), (0, 0)) + mm(split(st[1]), split(nr[1]), (0, 0)))

    @pl.when(diag & (q == 1))
    def _():
        for s in range(NS):
            q_loc[s] = mm(split(tiles[2 * s]), split(norm[s]), (0, 0))

    for s in range(NS):
        send(diag & (q == 1), lambda s=s: copy(q_loc.at[s], q_rx.at[s], q_s.at[1 + s], q_r.at[1 + s], sib))

    @pl.when(diag & (q == 1))
    def _():
        arrived(nr, g_r.at[2])
        for s in range(NS):
            value = mm(split(tiles[2 * s]), split(nr[s])) + mm(split(tiles[2 * s + 1]), split(norm[s]))
            for d in range(4):
                p_out[s, d] = value[:, d * LANES : (d + 1) * LANES]

    @pl.when(diag & (q == 0))
    def _():
        for s in range(NS):
            value = mm(split(tiles[2 * s]), split(norm[s]))
            arrived(q_rx.at[s], q_r.at[1 + s])
            for d in range(4):
                lanes = slice(d * LANES, (d + 1) * LANES)
                p_out[s, d] = value[:, lanes] + q_rx[s, :, lanes]

    send_slices(off, p_out.at[0], p_ss.at[0], s_own, r, c)
    for s in range(NS):
        send_slices(diag, p_out.at[s], p_ss.at[s], s, r, c)

    own_slot = diag | (lower & (c < 4)) | (upper & (c >= 4))
    total = None
    for m in range(NC):

        @pl.when(jnp.logical_not(own_slot & (c == m)))
        def _():
            arrived(c_rx.at[m], c_r.at[m])

        total = c_rx[m] if total is None else total + c_rx[m]
    column = -total
    c_all[c] = column
    for d in range(1, NC):
        to = (c + d) % NC
        send(True, lambda d=d, to=to: copy(c_all.at[c], c_all.at[c], ca_s.at[d], ca_r.at[c], (r, to)))

    part = mm(split(norm[cz]), split(column), (0, 0))
    for a in range(NA):
        d_part[a] = part[a * PIECE : (a + 1) * PIECE]
    for d in range(1, NA):
        to = (r + d) % NA
        send(True, lambda d=d, to=to: copy(d_part.at[to], d_rx.at[r], dp_s.at[d], dp_r.at[r], (to, c)))
    acc = base[pl.ds(pl.multiple_of(r * PIECE, PIECE), PIECE), :] - d_part[r]
    for d in range(1, NA):
        of = (r + d) % NA
        arrived(d_rx.at[of], dp_r.at[of])
        acc = acc - d_rx[of]
    d_all[r, c] = acc
    for d in range(1, NC):
        to = (c + d) % NC
        send(True, lambda d=d, to=to: copy(d_all.at[r, c], d_all.at[r, c], da_s.at[d], da_r.at[c], (r, to)))
    for d in range(1, NC):
        of = (c + d) % NC
        arrived(d_all.at[r, of], da_r.at[of])
    for d in range(1, NC):
        to = (r + 2 * d) % NA
        send(True, lambda d=d, to=to: copy(d_all.at[r], d_all.at[r], db_s.at[d], db_r.at[k], (to, c)))
    send(True, lambda: copy(d_all.at[r], d_all.at[r], dc_s.at[0], dc_r.at[k], sib))
    for d in range(1, NC):
        of = (r + 2 * d) % NA
        arrived(d_all.at[of], db_r.at[of // 2])
        send(True, lambda d=d, of=of: copy(d_all.at[of], d_all.at[of], dc_s.at[d], dc_r.at[of // 2], sib))
    for m in range(NC):
        arrived(d_all.at[2 * m + 1 - q], dc_r.at[m])
    for d in range(1, NC):
        of = (c + d) % NC
        arrived(c_all.at[of], ca_r.at[of])
    for cond, make in pending:
        pl.when(cond)(lambda make=make: make().wait_send())


def place(tile_list, tile_valid, c_all, d_all, column_out, diag_out):
    t = pl.program_id(0)
    r = lax.axis_index("row")
    for s in range(NS):
        here = (tile_list[s, r] == 4 * r + t) & (tile_valid[s, r] > 0)
        for j in range(4):
            lanes = slice((4 * s + j) * LANES, (4 * s + j + 1) * LANES)
            column_out[:, lanes] = jnp.where(here, c_all[4 * s + j], 0.0)
            for a in range(4):
                diag_out[s, a * PIECE : (a + 1) * PIECE, j * LANES : (j + 1) * LANES] = d_all[a, 4 * s + j]


def shards(inverse_front, factor, unit_lower, pivot_inverse, tile_list, tile_valid):
    smem = pl.BlockSpec(memory_space=pltpu.SMEM)
    vmem = pl.BlockSpec(memory_space=pltpu.VMEM)
    tiles, norm, base = pl.pallas_call(
        prepare,
        out_shape=(
            jax.ShapeDtypeStruct((4, B, B), F32),
            jax.ShapeDtypeStruct((NS, B, W), F32),
            jax.ShapeDtypeStruct((W, LANES), F32),
        ),
        in_specs=[smem, smem, pl.BlockSpec(memory_space=pl.ANY), vmem, vmem, vmem],
        out_specs=(vmem, vmem, vmem),
        scratch_shapes=[pltpu.SemaphoreType.DMA((4,))],
        name="prepare",
    )(tile_list, tile_valid, inverse_front, factor, unit_lower, pivot_inverse.reshape(NS, 1, W))

    dma = pltpu.SemaphoreType.DMA
    c_all, d_all = pl.pallas_call(
        exchange,
        out_shape=(
            jax.ShapeDtypeStruct((NC, B, LANES), F32),
            jax.ShapeDtypeStruct((NA, NC, PIECE, LANES), F32),
        ),
        in_specs=[vmem, vmem, vmem],
        out_specs=(vmem, vmem),
        scratch_shapes=[
            pltpu.VMEM((2, B, B), F32),
            pltpu.VMEM((2, B, W), F32),
            pltpu.VMEM((2, B, W), F32),
            pltpu.VMEM((2, B, W), F32),
            pltpu.VMEM((2, 4, B, LANES), F32),
            pltpu.VMEM((4, B, LANES), F32),
            pltpu.VMEM((NC, B, LANES), F32),
            pltpu.VMEM((NA, PIECE, LANES), F32),
            pltpu.VMEM((NA, PIECE, LANES), F32),
            dma((2,)), dma((2,)),
            dma((1,)), dma((2,)),
            dma((2,)), dma((3,)),
            dma((3,)), dma((3,)),
            dma((2, 4)), dma((4,)), dma((NC,)),
            dma((NC,)), dma((NC,)),
            dma((NA,)), dma((NA,)),
            dma((NC,)), dma((NC,)),
            dma((NC,)), dma((NC,)),
            dma((NC,)), dma((NC,)),
        ],
        compiler_params=pltpu.CompilerParams(has_side_effects=True),
        name="exchange",
    )(tiles, norm, base)

    whole = lambda shape: pl.BlockSpec(shape, lambda t: (0,) * len(shape))
    return pl.pallas_call(
        place,
        grid=(4,),
        out_shape=(
            jax.ShapeDtypeStruct((4 * B, NS * W), F32),
            jax.ShapeDtypeStruct((NS, W, W), F32),
        ),
        in_specs=[
            smem,
            smem,
            whole((NC, B, LANES)),
            pl.BlockSpec((4, NC, PIECE, LANES), lambda t: (t, 0, 0, 0)),
        ],
        out_specs=(
            pl.BlockSpec((B, NS * W), lambda t: (t, 0)),
            pl.BlockSpec((NS, W // 4, W), lambda t: (0, t, 0)),
        ),
        name="place",
    )(tile_list, tile_valid, c_all, d_all)


def solution(mesh):
    in_specs = (P("row", "col"), P("row", None), P(), P(), P(), P())
    out_specs = (P("row", None), P())
    return jax.shard_map(shards, mesh=mesh, in_specs=in_specs, out_specs=out_specs, check_vma=False)
```

time: 629 us -> 141 us (0.22); the launches traced: 621 us -> 141 us
  waiting for transfers between devices: 405 us -> 0 us
  Pallas kernels: 0 us -> 139 us
  matrix products: 129 us -> 0 us
  local copies, waits for them, and re-layouts: 61.2 us -> 1.28 us
  between operations: 14.2 us -> 0.65 us
  other arithmetic: 10.9 us -> 0 us
    psum x3 -> x0, waiting for transfers between devices: 310 us -> none  [the longest x1 116 us: shards(): diag_total = lax.psum(diag_terms, 'row')]
    pallas_call x0 -> x3, Pallas kernels: none -> 139 us  [the longest x1 128 us: shards(): pl.pallas_call(exchange, out_shape=(jax.ShapeDtypeStruct((NC, B, LANES),...]
    dot_general x10 -> x0, matrix products: 129 us -> none  [the longest x3 64.2 us: inner_left(): lax.dot_general(left, right, (((0,), (0,)), ((), ())), precision=lax.Prec...]
    all_gather x1 -> x0, waiting for transfers between devices: 95.2 us -> none  [shards(): normalized = lax.all_gather(normalize(factor), 'row', axis=0, tiled=True)]
    unnamed x20 -> x0, local copies, waits for them, and re-layouts: 28.9 us -> none
    reshape x1, local copies, waits for them, and re-layouts: 20.3 us -> 1.28 us  [shards(): pivot_inverse.reshape(NS, 1, W)]
    transpose x1 -> x0, local copies, waits for them, and re-layouts: 10.5 us -> none  [place_tiles(): jnp.einsum('sta,absw->tbsw', onehot, slot_tiles, precision=lax.Precision....]
  transfers between devices with their start and end apart: 4 -> 0, of which waited for: 4 -> 0; matrix products, arithmetic and copies ran while one was open for 10% -> 0% of each run, Pallas kernels for 0% -> 0%
where the time goes in v1:
time: 141 us
  Pallas kernels  139 us (99%)
    pallas_call x1, Pallas kernels, shards(): pl.pallas_call(exchange, out_shape=(jax.ShapeDtypeStruct((NC, B, LANES),...  128 us
    pallas_call x1, Pallas kernels, shards(): pl.pallas_call(prepare, out_shape=(jax.ShapeDtypeStruct((4, B, B), F32),...  5.47 us
    pallas_call x1, Pallas kernels, shards(): pl.pallas_call(place, grid=(4,), out_shape=(jax.ShapeDtypeStruct((4 * B,...  5.34 us

profile of v1, /device:TPU:1, one launch (start us, length us, event | category | flops | bytes accessed | tf_op | source)
XLA Modules:
  0.0 141.0 jit_solution(13655715234755199190)
XLA Ops:
  0.6 1.3 reshape.7.pivot
  1.9 5.5 %prepare.1 = (f32[4,256,256]{2,1,0:T(8,128)}, f32[2,256,512]{2,1,0:T(8,128)}, f32[512,128]{1,0:T(8,128)}) custom-call(s32[2,16]{1,0:T(2,128)} %tile_list.3, s32[2,16]{1,0:T(2,128)} %tile_valid.3, f32[1024,2048]{1,0:T(8,128)} %front.1, f32[256,1024]{1,0:T(8,128)} %factor.1, f32[2,512,512]{2,1,0:T(8,128)} %lower.1, f32[2,1,512]{2,1,0:T(1,128)} %reshape.7.pivot), custom_call_target="tpu_custom_call" | custom-call | tf_op jit(solution)/shard_map/prepare/pallas_call | solution.py:270
  7.4 128.2 %exchange.1 = (f32[8,256,128]{2,1,0:T(8,128)}, f32[16,8,32,128]{3,2,1,0:T(8,128)}) custom-call(f32[4,256,256]{2,1,0:T(8,128)} %get-tuple-element.7.tiles, f32[2,256,512]{2,1,0:T(8,128)} %get-tuple-element.8.norm, f32[512,128]{1,0:T(8,128)} %get-tuple-element.9.base), custom_call_target="tpu_custom_call" | custom-call | tf_op jit(solution)/shard_map/exchange/pallas_call | solution.py:284
  135.6 5.3 %place.1 = (f32[1024,1024]{1,0:T(8,128)}, f32[2,512,512]{2,1,0:T(8,128)}) custom-call(s32[2,16]{1,0:T(2,128)} %tile_list.3, s32[2,16]{1,0:T(2,128)} %tile_valid.3, f32[8,256,128]{2,1,0:T(8,128)} %get-tuple-element.10.c_all, f32[16,8,32,128]{3,2,1,0:T(8,128)} %get-tuple-element.11.d_all), custom_call_target="tpu_custom_call" | custom-call | tf_op jit(solution)/shard_map/place/pallas_call | solution.py:318

commit v2 on v1

--- a/solution.py
+++ b/solution.py
@@ -73,23 +73,51 @@
                 tiles_out[2 * s + j] = jnp.where(b0 >= b1, tile, tile.T)
 
 
+FULL = (
+    ((0, 1), (0, 1), (0, 0), (0, 0)),
+    ((0, 1), (1, 1), (0, 0), (0, 0)),
+    ((1, 0), (3, 1), (2, 0), (0, 1)),
+    ((2, 1), (0, 0), (1, 1), (1, 0)),
+)
+PAIRS0 = (
+    (1, 0, ((1, 0), (3, 0), (2, 0), (2, 1))),
+    (2, 0, ((2, 0), (1, 1), (3, 0), (0, 1))),
+    (3, 0, ((0, 0), (1, 0), (3, 0), (3, 1))),
+    (2, 1, ((2, 0), (3, 0), (2, 1), (1, 0))),
+    (3, 1, ((2, 0), (1, 1), (3, 1), (3, 0))),
+    (3, 2, ((3, 1), (1, 0), (3, 0), (3, 0))),
+)
+PAIRS3 = (
+    (1, 0, ((1, 1), (0, 1), (3, 1), (2, 1))),
+    (2, 0, ((2, 1), (1, 0), (1, 1), (0, 1))),
+    (3, 0, ((3, 1), (0, 0), (1, 1), (3, 0))),
+    (2, 1, ((0, 1), (3, 0), (2, 0), (2, 1))),
+    (3, 1, ((1, 1), (2, 1), (3, 1), (1, 0))),
+    (3, 2, ((0, 1), (2, 0), (3, 1), (1, 1))),
+)
+HALF = B // 2
+
+
 def exchange(
     tiles, norm, base, c_all, d_all,
-    st, nr, q_loc, q_rx, p_out, q_out, c_rx, d_part, d_rx,
-    st_s, st_r, n_s, n_r, g_s, g_r, q_s, q_r, p_ss, q_ss, c_r, ca_s, ca_r, dp_s, dp_r, da_s, da_r, db_s, db_r, dc_s, dc_r,
+    nr, q_loc, q_rx, p_out, q_out, cp_rx, cq_rx, p_sum, q_sum, pf_rx, qt_rx, d_part, d_rx,
+    n_s, n_r, g_s, g_r, q_s, q_r, p_ss, q_ss, cp_r, cq_r, f_s, f_r, t_s, t_r,
+    ca_s, ca_r, dp_s, dp_r, da_s, da_r, db_s, db_r, dc_s, dc_r,
 ):
     r = lax.axis_index("row")
     c = lax.axis_index("col")
     k = r // 2
     q = r % 2
-    cy = c % 4
-    cz = c // 4
+    x = k % 4
+    zl = k // 4
+    y = cy = c % 4
+    zh = cz = c // 4
     sib = (r + 1 - 2 * q, c)
     lower = k > c
-    upper = k < c
-    off = k != c
     diag = k == c
-    s_own = jnp.where(lower, 0, 1)
+    full = (zl == 1) & (zh == 0)
+    tri = zl == zh
+    work = full | tri
     pending = []
 
     def copy(src, dst, ssem, rsem, dev):
@@ -104,118 +132,143 @@
     def arrived(buf, sem):
         copy(buf, buf, sem, sem, sib).wait_recv()
 
-    for j in range(2):
-        send(lower, lambda j=j: copy(tiles.at[2 + j], st.at[q], st_s.at[j], st_r.at[q], (2 * c + j, k)))
-    send(off, lambda: copy(norm.at[1 - s_own], nr.at[q], n_s.at[0], n_r.at[q], (2 * c + q, k)))
-    send(diag & (q == 0), lambda: copy(norm, nr, g_s.at[0], g_r.at[2], sib))
-
-    def ship(slices, sems, s, row, slot):
+    def give(cond, j, sem, row, col):
+        part = pl.ds(j % 2 * HALF, HALF)
+        send(cond, lambda: copy(norm.at[j // 2, part], nr.at[q, j // 2, part], n_s.at[sem], n_r.at[j], (row, col)))
+
+    count = 0
+    for j in range(4):
         for d in range(4):
-            def make(d=d):
-                return copy(slices.at[d], c_rx.at[slot], sems.at[d], c_r.at[slot], (row, 4 * s + d))
-            yield d, make
-
-    def send_slices(cond, slices, sems, s, row, slot):
-        for d, make in ship(slices, sems, s, row, slot):
-            mine = (row == r) & (4 * s + d == c)
-            send(cond & jnp.logical_not(mine), make)
-
-            @pl.when(cond & mine)
-            def _():
-                c_rx[slot] = slices[d]
-
-    n_own = norm.at[s_own]
-
-    @pl.when(off)
-    def _():
-        own = split(n_own[...])
-        for j in range(2):
-
-            @pl.when(lower)
-            def _():
-                q_loc[j] = mm(split(tiles[j]), own, (0, 0))
-
-            @pl.when(upper)
-            def _():
-                arrived(st.at[j], st_r.at[j])
-                q_loc[j] = mm(split(st[j]), own)
-
-    send(off, lambda: copy(q_loc.at[1 - q], q_rx.at[0], q_s.at[0], q_r.at[0], sib))
-
-    @pl.when(off)
-    def _():
-        arrived(nr.at[q], n_r.at[q])
-
-    send(off, lambda: copy(nr.at[q], nr.at[q], g_s.at[1], g_r.at[q], sib))
-
-    @pl.when(off)
-    def _():
-        arrived(q_rx.at[0], q_r.at[0])
-        for d in range(4):
-            lanes = slice(d * LANES, (d + 1) * LANES)
-            q_out[d] = q_loc[q, :, lanes] + q_rx[0, :, lanes]
-
-    send_slices(off, q_out, q_ss, s_own, 2 * c + q, k)
-
-    @pl.when(off)
-    def _():
-        arrived(nr.at[1 - q], g_r.at[1 - q])
-
-        def put(value):
-            for d in range(4):
-                p_out[0, d] = value[:, d * LANES : (d + 1) * LANES]
-
-        @pl.when(lower)
-        def _():
-            put(mm(split(tiles[0]), split(nr[0])) + mm(split(tiles[1]), split(nr[1])))
-
-        @pl.when(upper)
-        def _():
-            put(mm(split(st[0]), split(nr[0]), (0, 0)) + mm(split(st[1]), split(nr[1]), (0, 0)))
+            alpha, side = FULL[d][j]
+            give((zl == 0) & (zh == side) & ((y - x + 4) % 4 == alpha), j, count, 8 + 2 * ((x + d) % 4) + q, x)
+            count += 1
+        for n, pairs in ((0, PAIRS0), (1, PAIRS3)):
+            for px, py, rule in pairs:
+                alpha, side = rule[j]
+                cond = (zl == n) & (zh == side) & (x == py) & (y == (py + alpha) % 4)
+                give(cond, j, count, 8 * n + 2 * px + q, 4 * n + py)
+                count += 1
+    send(diag & (q == 0), lambda: copy(norm, nr.at[0], g_s.at[0], g_r.at[0], sib))
+
+    @pl.when(lower)
+    def _():
+        for s in range(NS):
+            own = split(norm[s])
+            for j in range(2):
+                q_loc[j, s] = mm(split(tiles[2 * s + j]), own, (0, 0))
 
     @pl.when(diag & (q == 1))
     def _():
         for s in range(NS):
-            q_loc[s] = mm(split(tiles[2 * s]), split(norm[s]), (0, 0))
-
-    for s in range(NS):
-        send(diag & (q == 1), lambda s=s: copy(q_loc.at[s], q_rx.at[s], q_s.at[1 + s], q_r.at[1 + s], sib))
-
-    @pl.when(diag & (q == 1))
-    def _():
-        arrived(nr, g_r.at[2])
-        for s in range(NS):
-            value = mm(split(tiles[2 * s]), split(nr[s])) + mm(split(tiles[2 * s + 1]), split(norm[s]))
-            for d in range(4):
-                p_out[s, d] = value[:, d * LANES : (d + 1) * LANES]
-
-    @pl.when(diag & (q == 0))
-    def _():
-        for s in range(NS):
-            value = mm(split(tiles[2 * s]), split(norm[s]))
-            arrived(q_rx.at[s], q_r.at[1 + s])
+            q_loc[0, s] = mm(split(tiles[2 * s]), split(norm[s]), (0, 0))
+
+    give_q = lower | (diag & (q == 1))
+    send(give_q, lambda: copy(q_loc.at[jnp.where(lower, 1 - q, 0)], q_rx, q_s.at[0], q_r.at[0], sib))
+
+    @pl.when(lower | (diag & (q == 0)))
+    def _():
+        arrived(q_rx, q_r.at[0])
+
+    @pl.when(lower)
+    def _():
+        for s in range(NS):
             for d in range(4):
                 lanes = slice(d * LANES, (d + 1) * LANES)
-                p_out[s, d] = value[:, lanes] + q_rx[s, :, lanes]
-
-    send_slices(off, p_out.at[0], p_ss.at[0], s_own, r, c)
+                q_out[d, s] = q_loc[q, s, :, lanes] + q_rx[s, :, lanes]
+        cq_rx[x] = q_out[x]
+
+    for d in range(4):
+        send(lower & (x != d), lambda d=d: copy(q_out.at[d], cq_rx.at[x], q_ss.at[d], cq_r.at[x], (8 * zl + 2 * d + q, c)))
+
+    @pl.when(lower)
+    def _():
+        for j in range(4):
+            arrived(nr.at[q, j // 2, pl.ds(j % 2 * HALF, HALF)], n_r.at[j])
+
+    send(lower, lambda: copy(nr.at[q], nr.at[q], g_s.at[1], g_r.at[1], sib))
+
+    def put(s, value):
+        for d in range(4):
+            p_out[d, s] = value[:, d * LANES : (d + 1) * LANES]
+
+    @pl.when(lower)
+    def _():
+        arrived(nr.at[1 - q], g_r.at[1])
+        for s in range(NS):
+            put(s, mm(split(tiles[2 * s]), split(nr[0, s])) + mm(split(tiles[2 * s + 1]), split(nr[1, s])))
+
+    @pl.when(diag & (q == 1))
+    def _():
+        arrived(nr.at[0], g_r.at[0])
+        for s in range(NS):
+            put(s, mm(split(tiles[2 * s]), split(nr[0, s])) + mm(split(tiles[2 * s + 1]), split(norm[s])))
+
+    @pl.when(diag & (q == 0))
+    def _():
+        for s in range(NS):
+            put(s, mm(split(tiles[2 * s]), split(norm[s])) + q_rx[s])
+
+    @pl.when(lower | diag)
+    def _():
+        cp_rx[y] = p_out[y]
+
+    for d in range(4):
+        send((lower | diag) & (y != d), lambda d=d: copy(p_out.at[d], cp_rx.at[y], p_ss.at[d], cp_r.at[y], (r, 4 * zh + d)))
+
+    def gather(out, parts, sems, has, here):
+        out[...] = jnp.zeros_like(out)
+        for m in range(4):
+
+            @pl.when(has(m) & (here != m))
+            def _():
+                arrived(parts.at[m], sems.at[m])
+
+            @pl.when(has(m))
+            def _():
+                out[...] += parts[m]
+
+    gather(q_sum, cq_rx, cq_r, lambda m: full | (tri & (y < m)), x)
+    mirrored = full | (tri & (y < 3))
+    into = jnp.where(full, 1, 0)
     for s in range(NS):
-        send_slices(diag, p_out.at[s], p_ss.at[s], s, r, c)
-
-    own_slot = diag | (lower & (c < 4)) | (upper & (c >= 4))
-    total = None
-    for m in range(NC):
-
-        @pl.when(jnp.logical_not(own_slot & (c == m)))
+        row, col = 8 * zh + 2 * y + q, 4 * s + x
+        mine = (row == r) & (col == c)
+        send(
+            mirrored & jnp.logical_not(mine),
+            lambda s=s, row=row, col=col: copy(q_sum.at[s], qt_rx.at[into], t_s.at[s], t_r.at[into], (row, col)),
+        )
+
+        @pl.when(mirrored & mine)
         def _():
-            arrived(c_rx.at[m], c_r.at[m])
-
-        total = c_rx[m] if total is None else total + c_rx[m]
-    column = -total
+            qt_rx[0] = q_sum[s]
+
+    gather(p_sum, cp_rx, cp_r, lambda m: full | (tri & (x >= m)), y)
+    far = (c + 4) % NC
+    send(work, lambda: copy(p_sum.at[1 - zh], pf_rx, f_s.at[0], f_r.at[0], (r, far)))
+
+    total = p_sum.at[zh]
+    first = (zl == 0) & (zh == 0)
+
+    @pl.when(jnp.logical_not(first))
+    def _():
+        arrived(pf_rx, f_r.at[0])
+        total[...] += pf_rx[...]
+
+    @pl.when((x < 3) & jnp.logical_not(tri & (x == y)))
+    def _():
+        arrived(qt_rx.at[0], t_r.at[0])
+
+    @pl.when(x < 3)
+    def _():
+        total[...] += qt_rx[0]
+
+    @pl.when(zl == 0)
+    def _():
+        arrived(qt_rx.at[1], t_r.at[1])
+        total[...] += qt_rx[1]
+
+    column = -total[...]
     c_all[c] = column
-    for d in range(1, NC):
-        to = (c + d) % NC
-        send(True, lambda d=d, to=to: copy(c_all.at[c], c_all.at[c], ca_s.at[d], ca_r.at[c], (r, to)))
 
     part = mm(split(norm[cz]), split(column), (0, 0))
     for a in range(NA):
@@ -223,6 +276,7 @@
     for d in range(1, NA):
         to = (r + d) % NA
         send(True, lambda d=d, to=to: copy(d_part.at[to], d_rx.at[r], dp_s.at[d], dp_r.at[r], (to, c)))
+    send(True, lambda: copy(c_all.at[c], c_all.at[c], ca_s.at[0], ca_r.at[c], (r, far)))
     acc = base[pl.ds(pl.multiple_of(r * PIECE, PIECE), PIECE), :] - d_part[r]
     for d in range(1, NA):
         of = (r + d) % NA
@@ -232,22 +286,40 @@
     for d in range(1, NC):
         to = (c + d) % NC
         send(True, lambda d=d, to=to: copy(d_all.at[r, c], d_all.at[r, c], da_s.at[d], da_r.at[c], (r, to)))
+
+    def along_y(d):
+        return 4 * cz + (cy + d) % 4
+
+    def along_x(d):
+        return r - r % 8 + (r + 2 * d) % 8
+
+    for d in range(1, 4):
+        send(True, lambda d=d: copy(c_all.at[c], c_all.at[c], ca_s.at[d], ca_r.at[c], (r, along_y(d))))
     for d in range(1, NC):
         of = (c + d) % NC
         arrived(d_all.at[r, of], da_r.at[of])
-    for d in range(1, NC):
-        to = (r + 2 * d) % NA
-        send(True, lambda d=d, to=to: copy(d_all.at[r], d_all.at[r], db_s.at[d], db_r.at[k], (to, c)))
+    near = (r + 8) % NA
+    send(True, lambda: copy(d_all.at[r], d_all.at[r], db_s.at[0], db_r.at[k], (near, c)))
+    for d in range(1, 4):
+        send(True, lambda d=d: copy(d_all.at[r], d_all.at[r], db_s.at[d], db_r.at[k], (along_x(d), c)))
     send(True, lambda: copy(d_all.at[r], d_all.at[r], dc_s.at[0], dc_r.at[k], sib))
-    for d in range(1, NC):
-        of = (r + 2 * d) % NA
-        arrived(d_all.at[of], db_r.at[of // 2])
-        send(True, lambda d=d, of=of: copy(d_all.at[of], d_all.at[of], dc_s.at[d], dc_r.at[of // 2], sib))
+    arrived(c_all.at[far], ca_r.at[far])
+    for d in range(1, 4):
+        send(True, lambda d=d: copy(c_all.at[far], c_all.at[far], ca_s.at[3 + d], ca_r.at[far], (r, along_y(d))))
+    arrived(d_all.at[near], db_r.at[near // 2])
+    for d in range(1, 4):
+        send(True, lambda d=d: copy(d_all.at[near], d_all.at[near], db_s.at[3 + d], db_r.at[near // 2], (along_x(d), c)))
+    send(True, lambda: copy(d_all.at[near], d_all.at[near], dc_s.at[1], dc_r.at[near // 2], sib))
+    for h in range(2):
+        for d in range(1, 4):
+            of = (along_x(d) + 8 * h) % NA
+            arrived(d_all.at[of], db_r.at[of // 2])
+            send(True, lambda d=d, h=h, of=of: copy(d_all.at[of], d_all.at[of], dc_s.at[1 + 3 * h + d], dc_r.at[of // 2], sib))
+    for d in range(1, 4):
+        for of in (along_y(d), (along_y(d) + 4) % NC):
+            arrived(c_all.at[of], ca_r.at[of])
     for m in range(NC):
         arrived(d_all.at[2 * m + 1 - q], dc_r.at[m])
-    for d in range(1, NC):
-        of = (c + d) % NC
-        arrived(c_all.at[of], ca_r.at[of])
     for cond, make in pending:
         pl.when(cond)(lambda make=make: make().wait_send())
 
@@ -290,20 +362,25 @@
         in_specs=[vmem, vmem, vmem],
         out_specs=(vmem, vmem),
         scratch_shapes=[
-            pltpu.VMEM((2, B, B), F32),
-            pltpu.VMEM((2, B, W), F32),
-            pltpu.VMEM((2, B, W), F32),
-            pltpu.VMEM((2, B, W), F32),
-            pltpu.VMEM((2, 4, B, LANES), F32),
-            pltpu.VMEM((4, B, LANES), F32),
-            pltpu.VMEM((NC, B, LANES), F32),
+            pltpu.VMEM((2, NS, B, W), F32),
+            pltpu.VMEM((2, NS, B, W), F32),
+            pltpu.VMEM((NS, B, W), F32),
+            pltpu.VMEM((4, NS, B, LANES), F32),
+            pltpu.VMEM((4, NS, B, LANES), F32),
+            pltpu.VMEM((4, NS, B, LANES), F32),
+            pltpu.VMEM((4, NS, B, LANES), F32),
+            pltpu.VMEM((NS, B, LANES), F32),
+            pltpu.VMEM((NS, B, LANES), F32),
+            pltpu.VMEM((B, LANES), F32),
+            pltpu.VMEM((2, B, LANES), F32),
             pltpu.VMEM((NA, PIECE, LANES), F32),
             pltpu.VMEM((NA, PIECE, LANES), F32),
+            dma((64,)), dma((4,)),
             dma((2,)), dma((2,)),
-            dma((1,)), dma((2,)),
-            dma((2,)), dma((3,)),
-            dma((3,)), dma((3,)),
-            dma((2, 4)), dma((4,)), dma((NC,)),
+            dma((1,)), dma((1,)),
+            dma((4,)), dma((4,)), dma((4,)), dma((4,)),
+            dma((1,)), dma((1,)),
+            dma((2,)), dma((2,)),
             dma((NC,)), dma((NC,)),
             dma((NA,)), dma((NA,)),
             dma((NC,)), dma((NC,)),

time: 141 us -> 106 us (0.75)
  Pallas kernels: 139 us -> 104 us
    pallas_call x1, Pallas kernels: 128 us -> 93.1 us  [shards(): pl.pallas_call(exchange, out_shape=(jax.ShapeDtypeStruct((NC, B, LANES),...]
where the time goes in v2:
time: 106 us
  Pallas kernels  104 us (98%)
  local copies, waits for them, and re-layouts  1.28 us (1%)
    pallas_call x1, Pallas kernels, shards(): pl.pallas_call(exchange, out_shape=(jax.ShapeDtypeStruct((NC, B, LANES),...  93.1 us
    pallas_call x1, Pallas kernels, shards(): pl.pallas_call(prepare, out_shape=(jax.ShapeDtypeStruct((4, B, B), F32),...  5.47 us
    pallas_call x1, Pallas kernels, shards(): pl.pallas_call(place, grid=(4,), out_shape=(jax.ShapeDtypeStruct((4 * B,...  5.33 us

profile of v2, /device:TPU:1, one launch (start us, length us, event | category | flops | bytes accessed | tf_op | source)
XLA Modules:
  0.0 105.8 jit_solution(4571173781065702571)
XLA Ops:
  0.6 1.3 %reshape.7.pivot = f32[2,1,512]{2,1,0:T(1,128)} reshape(f32[2,512]{1,0:T(2,128)} %param.9) | data formatting | bytes 8192 | tf_op jit(solution)/shard_map/reshape | solution.py:353
  1.9 5.5 %prepare.1 = (f32[4,256,256]{2,1,0:T(8,128)}, f32[2,256,512]{2,1,0:T(8,128)}, f32[512,128]{1,0:T(8,128)}) custom-call(s32[2,16]{1,0:T(2,128)} %tile_list.3, s32[2,16]{1,0:T(2,128)} %tile_valid.3, f32[1024,2048]{1,0:T(8,128)} %front.1, f32[256,1024]{1,0:T(8,128)} %factor.1, f32[2,512,512]{2,1,0:T(8,128)} %lower.1, f32[2,1,512]{2,1,0:T(1,128)} %reshape.7.pivot), custom_call_target="tpu_custom_call" | custom-call | tf_op jit(solution)/shard_map/prepare/pallas_call | solution.py:342
  7.4 93.1 %exchange.1 = (f32[8,256,128]{2,1,0:T(8,128)}, f32[16,8,32,128]{3,2,1,0:T(8,128)}) custom-call(f32[4,256,256]{2,1,0:T(8,128)} %get-tuple-element.7.tiles, f32[2,256,512]{2,1,0:T(8,128)} %get-tuple-element.8.norm, f32[512,128]{1,0:T(8,128)} %get-tuple-element.9.base), custom_call_target="tpu_custom_call" | custom-call | tf_op jit(solution)/shard_map/exchange/pallas_call | solution.py:356
  100.5 5.3 %place.1 = (f32[1024,1024]{1,0:T(8,128)}, f32[2,512,512]{2,1,0:T(8,128)}) custom-call(s32[2,16]{1,0:T(2,128)} %tile_list.3, s32[2,16]{1,0:T(2,128)} %tile_valid.3, f32[8,256,128]{2,1,0:T(8,128)} %get-tuple-element.10.c_all, f32[16,8,32,128]{3,2,1,0:T(8,128)} %get-tuple-element.11.d_all), custom_call_target="tpu_custom_call" | custom-call | tf_op jit(solution)/shard_map/place/pallas_call | solution.py:395

commit v3 on v2

--- a/solution.py
+++ b/solution.py
@@ -27,50 +27,6 @@
         return lax.dot_general(x, y, (((dims[0],), (dims[1],)), ((), ())), preferred_element_type=F32)
 
     return dot(a[0], b[0]) + (dot(a[0], b[1]) + dot(a[1], b[0]))
-
-
-def prepare(tile_list, tile_valid, front, factor, lower, pivot, tiles_out, norm_out, base_out, sems):
-    r = lax.axis_index("row")
-    c = lax.axis_index("col")
-    copies = []
-    for s in range(NS):
-        for j in range(2):
-            row = (tile_list[s, r] - 4 * r) * B
-            col = (tile_list[s, 2 * c + j] - 8 * c) * B
-            src = front.at[pl.ds(pl.multiple_of(row, B), B), pl.ds(pl.multiple_of(col, B), B)]
-            copies.append(pltpu.make_async_copy(src, tiles_out.at[2 * s + j], sems.at[2 * s + j]))
-    for copy in copies:
-        copy.start()
-    i0 = lax.broadcasted_iota(jnp.int32, (W, W), 0)
-    i1 = lax.broadcasted_iota(jnp.int32, (W, W), 1)
-    for s in range(NS):
-        inv = jnp.where(i0 > i1, lower[s], jnp.where(i0 == i1, 1.0, 0.0))
-        keep = (tile_valid[s, r] > 0).astype(F32)
-        fac = factor[:, s * W : (s + 1) * W] * keep
-        inv_split = split(inv)
-        norm_out[s] = mm(split(fac), inv_split)
-
-        @pl.when(c // 4 == s)
-        def _():
-            i2 = lax.broadcasted_iota(jnp.int32, (W, LANES), 0)
-            i3 = lax.broadcasted_iota(jnp.int32, (W, LANES), 1) + (c % 4) * LANES
-            lanes = pl.ds(pl.multiple_of((c % 4) * LANES, LANES), LANES)
-            part = jnp.where(i2 > i3, lower[s, :, lanes], jnp.where(i2 == i3, 1.0, 0.0))
-            scaled = part * pivot[s].T
-            base_out[...] = mm(inv_split, split(scaled), (0, 0))
-
-    for copy in copies:
-        copy.wait()
-    own = r - 2 * c
-    b0 = lax.broadcasted_iota(jnp.int32, (B, B), 0)
-    b1 = lax.broadcasted_iota(jnp.int32, (B, B), 1)
-    for j in range(2):
-
-        @pl.when(own == j)
-        def _():
-            for s in range(NS):
-                tile = tiles_out[2 * s + j]
-                tiles_out[2 * s + j] = jnp.where(b0 >= b1, tile, tile.T)
 
 
 FULL = (
@@ -99,8 +55,8 @@
 
 
 def exchange(
-    tiles, norm, base, c_all, d_all,
-    nr, q_loc, q_rx, p_out, q_out, cp_rx, cq_rx, p_sum, q_sum, pf_rx, qt_rx, d_part, d_rx,
+    tile_list, tile_valid, front_hbm, factor_hbm, lower_hbm, pivot_hbm, c_all, d_all,
+    front, factor, lower_v, pivot, tiles, norm, base, in_s, nr, q_loc, q_rx, p_out, q_out, cp_rx, cq_rx, p_sum, q_sum, pf_rx, qt_rx, d_part, d_rx,
     n_s, n_r, g_s, g_r, q_s, q_r, p_ss, q_ss, cp_r, cq_r, f_s, f_r, t_s, t_r,
     ca_s, ca_r, dp_s, dp_r, da_s, da_r, db_s, db_r, dc_s, dc_r,
 ):
@@ -132,6 +88,44 @@
     def arrived(buf, sem):
         copy(buf, buf, sem, sem, sib).wait_recv()
 
+    fetch = [
+        pltpu.make_async_copy(factor_hbm, factor, in_s.at[0]),
+        pltpu.make_async_copy(lower_hbm, lower_v, in_s.at[1]),
+        pltpu.make_async_copy(pivot_hbm, pivot, in_s.at[2]),
+    ]
+    for item in fetch:
+        item.start()
+
+    @pl.when(lower | diag)
+    def _():
+        for i in range(4):
+            for j in range(8):
+                part = front_hbm.at[i * B : (i + 1) * B, j * B : (j + 1) * B]
+                pltpu.make_async_copy(part, front.at[i, j], in_s.at[3]).start()
+
+    entry = pltpu.get_barrier_semaphore()
+
+    def greet(cond, dev):
+        pl.when(cond)(lambda: pl.semaphore_signal(entry, inc=1, device_id=dev, device_id_type=MESH))
+
+    for d in range(1, NC):
+        greet(True, (r, (c + d) % NC))
+    for d in range(1, NA):
+        greet(True, ((r + d) % NA, c))
+    for m in range(NC):
+        greet(jnp.logical_not(diag & (c == m)), (2 * c + q, m))
+        greet(jnp.logical_not(diag & (k == m)), (2 * m + q, k))
+
+    i0 = lax.broadcasted_iota(jnp.int32, (W, W), 0)
+    i1 = lax.broadcasted_iota(jnp.int32, (W, W), 1)
+    fetch[0].wait()
+    fetch[1].wait()
+    for s in range(NS):
+        inv = jnp.where(i0 > i1, lower_v[s], jnp.where(i0 == i1, 1.0, 0.0))
+        keep = (tile_valid[s, r] > 0).astype(F32)
+        norm[s] = mm(split(factor[:, s * W : (s + 1) * W] * keep), split(inv))
+    pl.semaphore_wait(entry, jnp.where(diag, 36, 38))
+
     def give(cond, j, sem, row, col):
         part = pl.ds(j % 2 * HALF, HALF)
         send(cond, lambda: copy(norm.at[j // 2, part], nr.at[q, j // 2, part], n_s.at[sem], n_r.at[j], (row, col)))
@@ -150,6 +144,20 @@
                 count += 1
     send(diag & (q == 0), lambda: copy(norm, nr.at[0], g_s.at[0], g_r.at[0], sib))
 
+    @pl.when(lower | diag)
+    def _():
+        pltpu.make_async_copy(front, front, in_s.at[3]).wait()
+        b0 = lax.broadcasted_iota(jnp.int32, (B, B), 0)
+        b1 = lax.broadcasted_iota(jnp.int32, (B, B), 1)
+        for s in range(NS):
+            for j in range(2):
+                tiles[2 * s + j] = front[lax.rem(tile_list[s, r], 4), lax.rem(tile_list[s, 2 * c + j], 8)]
+
+                @pl.when(r == 2 * c + j)
+                def _():
+                    tile = tiles[2 * s + j]
+                    tiles[2 * s + j] = jnp.where(b0 >= b1, tile, tile.T)
+
     @pl.when(lower)
     def _():
         for s in range(NS):
@@ -179,6 +187,18 @@
 
     for d in range(4):
         send(lower & (x != d), lambda d=d: copy(q_out.at[d], cq_rx.at[x], q_ss.at[d], cq_r.at[x], (8 * zl + 2 * d + q, c)))
+
+    fetch[2].wait()
+    for s in range(NS):
+
+        @pl.when(zh == s)
+        def _():
+            i2 = lax.broadcasted_iota(jnp.int32, (W, LANES), 0)
+            i3 = lax.broadcasted_iota(jnp.int32, (W, LANES), 1) + cy * LANES
+            lanes = pl.ds(pl.multiple_of(cy * LANES, LANES), LANES)
+            inv = jnp.where(i0 > i1, lower_v[s], jnp.where(i0 == i1, 1.0, 0.0))
+            part = jnp.where(i2 > i3, lower_v[s, :, lanes], jnp.where(i2 == i3, 1.0, 0.0))
+            base[...] = mm(split(inv), split(part * pivot[s : s + 1].T), (0, 0))
 
     @pl.when(lower)
     def _():
@@ -324,44 +344,62 @@
         pl.when(cond)(lambda make=make: make().wait_send())
 
 
-def place(tile_list, tile_valid, c_all, d_all, column_out, diag_out):
-    t = pl.program_id(0)
+def place(tile_list, tile_valid, c_all, d_all, column_out, diag_out, zeros, cols, block, out_s, d_s):
     r = lax.axis_index("row")
-    for s in range(NS):
-        here = (tile_list[s, r] == 4 * r + t) & (tile_valid[s, r] > 0)
-        for j in range(4):
-            lanes = slice((4 * s + j) * LANES, (4 * s + j + 1) * LANES)
-            column_out[:, lanes] = jnp.where(here, c_all[4 * s + j], 0.0)
-            for a in range(4):
-                diag_out[s, a * PIECE : (a + 1) * PIECE, j * LANES : (j + 1) * LANES] = d_all[a, 4 * s + j]
+    zeros[...] = jnp.zeros_like(zeros)
+
+    def out(src, s, t):
+        row = pl.ds(pl.multiple_of(t * B, B), B)
+        return pltpu.make_async_copy(src, column_out.at[row, s * W : (s + 1) * W], out_s.at[s, t])
+
+    live = [tile_valid[s, r] > 0 for s in range(NS)]
+    chosen = [tile_list[s, r] - 4 * r for s in range(NS)]
+    for s in range(NS):
+        for t in range(4):
+            pl.when(jnp.logical_not(live[s] & (chosen[s] == t)))(lambda s=s, t=t: out(zeros, s, t).start())
+    for s in range(NS):
+        for i in range(4):
+            cols[s, :, i * LANES : (i + 1) * LANES] = c_all[4 * s + i]
+        for t in range(4):
+            pl.when(live[s] & (chosen[s] == t))(lambda s=s, t=t: out(cols.at[s], s, t).start())
+    writes = []
+    for g in range(4):
+        rows = slice(4 * g * PIECE, 4 * (g + 1) * PIECE)
+        for a in range(4 * g, 4 * g + 4):
+            for i in range(NC):
+                lanes = slice(i % 4 * LANES, (i % 4 + 1) * LANES)
+                block[i // 4, a * PIECE : (a + 1) * PIECE, lanes] = d_all[a, i]
+        writes.append(pltpu.make_async_copy(block.at[:, rows], diag_out.at[:, rows], d_s.at[g]))
+        writes[-1].start()
+    for write in writes:
+        write.wait()
+    for s in range(NS):
+        for t in range(4):
+            out(zeros, s, t).wait()
 
 
 def shards(inverse_front, factor, unit_lower, pivot_inverse, tile_list, tile_valid):
     smem = pl.BlockSpec(memory_space=pltpu.SMEM)
     vmem = pl.BlockSpec(memory_space=pltpu.VMEM)
-    tiles, norm, base = pl.pallas_call(
-        prepare,
-        out_shape=(
-            jax.ShapeDtypeStruct((4, B, B), F32),
-            jax.ShapeDtypeStruct((NS, B, W), F32),
-            jax.ShapeDtypeStruct((W, LANES), F32),
-        ),
-        in_specs=[smem, smem, pl.BlockSpec(memory_space=pl.ANY), vmem, vmem, vmem],
-        out_specs=(vmem, vmem, vmem),
-        scratch_shapes=[pltpu.SemaphoreType.DMA((4,))],
-        name="prepare",
-    )(tile_list, tile_valid, inverse_front, factor, unit_lower, pivot_inverse.reshape(NS, 1, W))
-
+    hbm = pl.BlockSpec(memory_space=pl.ANY)
     dma = pltpu.SemaphoreType.DMA
     c_all, d_all = pl.pallas_call(
         exchange,
         out_shape=(
-            jax.ShapeDtypeStruct((NC, B, LANES), F32),
-            jax.ShapeDtypeStruct((NA, NC, PIECE, LANES), F32),
+            pltpu.VMEM((NC, B, LANES), F32),
+            pltpu.VMEM((NA, NC, PIECE, LANES), F32),
         ),
-        in_specs=[vmem, vmem, vmem],
+        in_specs=[smem, smem, hbm, hbm, hbm, hbm],
         out_specs=(vmem, vmem),
         scratch_shapes=[
+            pltpu.VMEM((4, 8, B, B), F32),
+            pltpu.VMEM((B, NS * W), F32),
+            pltpu.VMEM((NS, W, W), F32),
+            pltpu.VMEM((NS, W), F32),
+            pltpu.VMEM((2 * NS, B, B), F32),
+            pltpu.VMEM((NS, B, W), F32),
+            pltpu.VMEM((W, LANES), F32),
+            dma((4,)),
             pltpu.VMEM((2, NS, B, W), F32),
             pltpu.VMEM((2, NS, B, W), F32),
             pltpu.VMEM((NS, B, W), F32),
@@ -387,30 +425,32 @@
             dma((NC,)), dma((NC,)),
             dma((NC,)), dma((NC,)),
         ],
-        compiler_params=pltpu.CompilerParams(has_side_effects=True),
+        compiler_params=pltpu.CompilerParams(has_side_effects=True, collective_id=0),
         name="exchange",
-    )(tiles, norm, base)
-
-    whole = lambda shape: pl.BlockSpec(shape, lambda t: (0,) * len(shape))
+    )(tile_list, tile_valid, inverse_front, factor, unit_lower, pivot_inverse)
+
     return pl.pallas_call(
         place,
-        grid=(4,),
         out_shape=(
             jax.ShapeDtypeStruct((4 * B, NS * W), F32),
             jax.ShapeDtypeStruct((NS, W, W), F32),
         ),
-        in_specs=[
-            smem,
-            smem,
-            whole((NC, B, LANES)),
-            pl.BlockSpec((4, NC, PIECE, LANES), lambda t: (t, 0, 0, 0)),
+        in_specs=[smem, smem, vmem, vmem],
+        out_specs=(hbm, hbm),
+        scratch_shapes=[
+            pltpu.VMEM((B, W), F32),
+            pltpu.VMEM((NS, B, W), F32),
+            pltpu.VMEM((NS, W, W), F32),
+            dma((NS, 4)),
+            dma((4,)),
         ],
-        out_specs=(
-            pl.BlockSpec((B, NS * W), lambda t: (t, 0)),
-            pl.BlockSpec((NS, W // 4, W), lambda t: (0, t, 0)),
-        ),
         name="place",
-    )(tile_list, tile_valid, c_all, d_all)
+    )(
+        tile_list,
+        tile_valid,
+        pltpu.with_memory_space_constraint(c_all, pltpu.VMEM),
+        pltpu.with_memory_space_constraint(d_all, pltpu.VMEM),
+    )
 
 
 def solution(mesh):

time: 106 us -> 89.9 us (0.85)
  Pallas kernels: 104 us -> 89.1 us
  local copies, waits for them, and re-layouts: 1.28 us -> 0 us
    pallas_call x3 -> x2, Pallas kernels: 104 us -> 89.1 us  [the longest x1 85.6 us: shards(): pl.pallas_call(exchange, out_shape=(pltpu.VMEM((NC, B, LANES), F32), pltp...]
    reshape x1 -> x0, local copies, waits for them, and re-layouts: 1.28 us -> none  [shards(): pivot_inverse.reshape(NS, 1, W)]
where the time goes in v3:
time: 89.9 us; the launch traced here: 89.8 us
  Pallas kernels  89.1 us (99%)
    pallas_call x1, Pallas kernels, shards(): pl.pallas_call(exchange, out_shape=(pltpu.VMEM((NC, B, LANES), F32), pltp...  85.6 us
    pallas_call x1, Pallas kernels, shards(): pl.pallas_call(place, out_shape=(jax.ShapeDtypeStruct((4 * B, NS * W), F3...  3.52 us

profile of v3, /device:TPU:1, one launch (start us, length us, event | category | flops | bytes accessed | tf_op | source)
XLA Modules:
  0.0 89.8 jit_solution(3654530458961016967)
XLA Ops:
  0.6 85.6 %exchange.1 = (f32[8,256,128]{2,1,0:T(8,128)S(1)}, f32[16,8,32,128]{3,2,1,0:T(8,128)S(1)}) custom-call(s32[2,16]{1,0:T(2,128)} %tile_list.3, s32[2,16]{1,0:T(2,128)} %tile_valid.3, f32[1024,2048]{1,0:T(8,128)} %front_hbm.1, f32[256,1024]{1,0:T(8,128)} %factor_hbm.1, f32[2,512,512]{2,1,0:T(8,128)} %lower_hbm.1, f32[2,512]{1,0:T(2,128)} %pivot_hbm.1), custom_call_target="tpu_custom_call" | custom-call | tf_op jit(solution)/shard_map/exchange/pallas_call | solution.py:386
  86.2 3.5 %place.1 = (f32[1024,1024]{1,0:T(8,128)}, f32[2,512,512]{2,1,0:T(8,128)}) custom-call(s32[2,16]{1,0:T(2,128)} %tile_list.3, s32[2,16]{1,0:T(2,128)} %tile_valid.3, f32[8,256,128]{2,1,0:T(8,128)S(1)} %get-tuple-element.4.c_all, f32[16,8,32,128]{3,2,1,0:T(8,128)S(1)} %get-tuple-element.5.d_all), custom_call_target="tpu_custom_call" | custom-call | tf_op jit(solution)/shard_map/place/pallas_call | solution.py:432

commit v4 on v3

--- a/solution.py
+++ b/solution.py
@@ -30,26 +30,26 @@
 
 
 FULL = (
-    ((0, 1), (0, 1), (0, 0), (0, 0)),
-    ((0, 1), (1, 1), (0, 0), (0, 0)),
-    ((1, 0), (3, 1), (2, 0), (0, 1)),
-    ((2, 1), (0, 0), (1, 1), (1, 0)),
+    ((0, 0), (0, 1), (0, 1), (0, 0)),
+    ((0, 0), (2, 1), (1, 1), (1, 0)),
+    ((2, 1), (1, 1), (2, 0), (1, 0)),
+    ((3, 0), (2, 0), (2, 1), (3, 1)),
 )
 PAIRS0 = (
-    (1, 0, ((1, 0), (3, 0), (2, 0), (2, 1))),
-    (2, 0, ((2, 0), (1, 1), (3, 0), (0, 1))),
-    (3, 0, ((0, 0), (1, 0), (3, 0), (3, 1))),
-    (2, 1, ((2, 0), (3, 0), (2, 1), (1, 0))),
-    (3, 1, ((2, 0), (1, 1), (3, 1), (3, 0))),
-    (3, 2, ((3, 1), (1, 0), (3, 0), (3, 0))),
+    (1, 0, ((3, 0), (3, 1))),
+    (2, 0, ((0, 1), (0, 0))),
+    (3, 0, ((0, 1), (0, 0))),
+    (2, 1, ((0, 1), (2, 0))),
+    (3, 1, ((0, 1), (0, 0))),
+    (3, 2, ((3, 0), (0, 1))),
 )
 PAIRS3 = (
-    (1, 0, ((1, 1), (0, 1), (3, 1), (2, 1))),
-    (2, 0, ((2, 1), (1, 0), (1, 1), (0, 1))),
-    (3, 0, ((3, 1), (0, 0), (1, 1), (3, 0))),
-    (2, 1, ((0, 1), (3, 0), (2, 0), (2, 1))),
-    (3, 1, ((1, 1), (2, 1), (3, 1), (1, 0))),
-    (3, 2, ((0, 1), (2, 0), (3, 1), (1, 1))),
+    (1, 0, ((1, 1), (0, 1))),
+    (2, 0, ((3, 1), (0, 0))),
+    (3, 0, ((0, 1), (3, 1))),
+    (2, 1, ((3, 1), (0, 1))),
+    (3, 1, ((1, 1), (0, 1))),
+    (3, 2, ((1, 1), (0, 1))),
 )
 HALF = B // 2
 
@@ -58,7 +58,7 @@
     tile_list, tile_valid, front_hbm, factor_hbm, lower_hbm, pivot_hbm, c_all, d_all,
     front, factor, lower_v, pivot, tiles, norm, base, in_s, nr, q_loc, q_rx, p_out, q_out, cp_rx, cq_rx, p_sum, q_sum, pf_rx, qt_rx, d_part, d_rx,
     n_s, n_r, g_s, g_r, q_s, q_r, p_ss, q_ss, cp_r, cq_r, f_s, f_r, t_s, t_r,
-    ca_s, ca_r, dp_s, dp_r, da_s, da_r, db_s, db_r, dc_s, dc_r,
+    ca_s, ca_r, dp_s, dp_r, da_s, da_r, db_s, db_r, dh_s, dh_r, dc_s, dc_r,
 ):
     r = lax.axis_index("row")
     c = lax.axis_index("col")
@@ -126,21 +126,22 @@
         norm[s] = mm(split(factor[:, s * W : (s + 1) * W] * keep), split(inv))
     pl.semaphore_wait(entry, jnp.where(diag, 36, 38))
 
-    def give(cond, j, sem, row, col):
-        part = pl.ds(j % 2 * HALF, HALF)
-        send(cond, lambda: copy(norm.at[j // 2, part], nr.at[q, j // 2, part], n_s.at[sem], n_r.at[j], (row, col)))
+    def give(cond, s, part, sem, arrival, row, col):
+        send(cond, lambda: copy(norm.at[s, part], nr.at[q, s, part], n_s.at[sem], n_r.at[arrival], (row, col)))
 
     count = 0
-    for j in range(4):
-        for d in range(4):
-            alpha, side = FULL[d][j]
-            give((zl == 0) & (zh == side) & ((y - x + 4) % 4 == alpha), j, count, 8 + 2 * ((x + d) % 4) + q, x)
-            count += 1
+    for s in range(NS):
+        for j in (2 * s, 2 * s + 1):
+            for d in range(4):
+                alpha, side = FULL[d][j]
+                cond = (zl == 0) & (zh == side) & ((y - x + 4) % 4 == alpha)
+                give(cond, s, pl.ds(j % 2 * HALF, HALF), count, j, 8 + 2 * ((x + d) % 4) + q, x)
+                count += 1
         for n, pairs in ((0, PAIRS0), (1, PAIRS3)):
             for px, py, rule in pairs:
-                alpha, side = rule[j]
+                alpha, side = rule[s]
                 cond = (zl == n) & (zh == side) & (x == py) & (y == (py + alpha) % 4)
-                give(cond, j, count, 8 * n + 2 * px + q, 4 * n + py)
+                give(cond, s, pl.ds(0, B), count, 2 * s, 8 * n + 2 * px + q, 4 * n + py)
                 count += 1
     send(diag & (q == 0), lambda: copy(norm, nr.at[0], g_s.at[0], g_r.at[0], sib))
 
@@ -200,40 +201,44 @@
             part = jnp.where(i2 > i3, lower_v[s, :, lanes], jnp.where(i2 == i3, 1.0, 0.0))
             base[...] = mm(split(inv), split(part * pivot[s : s + 1].T), (0, 0))
 
-    @pl.when(lower)
-    def _():
-        for j in range(4):
-            arrived(nr.at[q, j // 2, pl.ds(j % 2 * HALF, HALF)], n_r.at[j])
-
-    send(lower, lambda: copy(nr.at[q], nr.at[q], g_s.at[1], g_r.at[1], sib))
-
-    def put(s, value):
+    for s in range(NS):
+
+        @pl.when(full)
+        def _():
+            for j in (2 * s, 2 * s + 1):
+                arrived(nr.at[q, s, pl.ds(j % 2 * HALF, HALF)], n_r.at[j])
+
+        @pl.when(lower & tri)
+        def _():
+            arrived(nr.at[q, s], n_r.at[2 * s])
+
+        send(lower, lambda s=s: copy(nr.at[q, s], nr.at[q, s], g_s.at[1 + s], g_r.at[1 + s], sib))
+
+        def put(value):
+            for d in range(4):
+                p_out[s, d] = value[:, d * LANES : (d + 1) * LANES]
+            cp_rx[s, y] = p_out[s, y]
+
+        @pl.when(lower)
+        def _():
+            arrived(nr.at[1 - q, s], g_r.at[1 + s])
+            put(mm(split(tiles[2 * s]), split(nr[0, s])) + mm(split(tiles[2 * s + 1]), split(nr[1, s])))
+
+        @pl.when(diag & (q == 1))
+        def _():
+            if s == 0:
+                arrived(nr.at[0], g_r.at[0])
+            put(mm(split(tiles[2 * s]), split(nr[0, s])) + mm(split(tiles[2 * s + 1]), split(norm[s])))
+
+        @pl.when(diag & (q == 0))
+        def _():
+            put(mm(split(tiles[2 * s]), split(norm[s])) + q_rx[s])
+
         for d in range(4):
-            p_out[d, s] = value[:, d * LANES : (d + 1) * LANES]
-
-    @pl.when(lower)
-    def _():
-        arrived(nr.at[1 - q], g_r.at[1])
-        for s in range(NS):
-            put(s, mm(split(tiles[2 * s]), split(nr[0, s])) + mm(split(tiles[2 * s + 1]), split(nr[1, s])))
-
-    @pl.when(diag & (q == 1))
-    def _():
-        arrived(nr.at[0], g_r.at[0])
-        for s in range(NS):
-            put(s, mm(split(tiles[2 * s]), split(nr[0, s])) + mm(split(tiles[2 * s + 1]), split(norm[s])))
-
-    @pl.when(diag & (q == 0))
-    def _():
-        for s in range(NS):
-            put(s, mm(split(tiles[2 * s]), split(norm[s])) + q_rx[s])
-
-    @pl.when(lower | diag)
-    def _():
-        cp_rx[y] = p_out[y]
-
-    for d in range(4):
-        send((lower | diag) & (y != d), lambda d=d: copy(p_out.at[d], cp_rx.at[y], p_ss.at[d], cp_r.at[y], (r, 4 * zh + d)))
+            send(
+                (lower | diag) & (y != d),
+                lambda s=s, d=d: copy(p_out.at[s, d], cp_rx.at[s, y], p_ss.at[s, d], cp_r.at[s, y], (r, 4 * zh + d)),
+            )
 
     def gather(out, parts, sems, has, here):
         out[...] = jnp.zeros_like(out)
@@ -262,9 +267,10 @@
         def _():
             qt_rx[0] = q_sum[s]
 
-    gather(p_sum, cp_rx, cp_r, lambda m: full | (tri & (x >= m)), y)
     far = (c + 4) % NC
-    send(work, lambda: copy(p_sum.at[1 - zh], pf_rx, f_s.at[0], f_r.at[0], (r, far)))
+    for s in range(NS):
+        gather(p_sum.at[s], cp_rx.at[s], cp_r.at[s], lambda m: full | (tri & (x >= m)), y)
+        send(work & (zh == 1 - s), lambda s=s: copy(p_sum.at[s], pf_rx, f_s.at[0], f_r.at[0], (r, far)))
 
     total = p_sum.at[zh]
     first = (zl == 0) & (zh == 0)
@@ -296,7 +302,14 @@
     for d in range(1, NA):
         to = (r + d) % NA
         send(True, lambda d=d, to=to: copy(d_part.at[to], d_rx.at[r], dp_s.at[d], dp_r.at[r], (to, c)))
-    send(True, lambda: copy(c_all.at[c], c_all.at[c], ca_s.at[0], ca_r.at[c], (r, far)))
+    def along_y(d):
+        return 4 * cz + (cy + d) % 4
+
+    def along_x(d):
+        return r - r % 8 + (r + 2 * d) % 8
+
+    for d in range(1, 4):
+        send(True, lambda d=d: copy(c_all.at[c], c_all.at[c], ca_s.at[d], ca_r.at[c], (r, along_y(d))))
     acc = base[pl.ds(pl.multiple_of(r * PIECE, PIECE), PIECE), :] - d_part[r]
     for d in range(1, NA):
         of = (r + d) % NA
@@ -307,14 +320,6 @@
         to = (c + d) % NC
         send(True, lambda d=d, to=to: copy(d_all.at[r, c], d_all.at[r, c], da_s.at[d], da_r.at[c], (r, to)))
 
-    def along_y(d):
-        return 4 * cz + (cy + d) % 4
-
-    def along_x(d):
-        return r - r % 8 + (r + 2 * d) % 8
-
-    for d in range(1, 4):
-        send(True, lambda d=d: copy(c_all.at[c], c_all.at[c], ca_s.at[d], ca_r.at[c], (r, along_y(d))))
     for d in range(1, NC):
         of = (c + d) % NC
         arrived(d_all.at[r, of], da_r.at[of])
@@ -322,19 +327,28 @@
     send(True, lambda: copy(d_all.at[r], d_all.at[r], db_s.at[0], db_r.at[k], (near, c)))
     for d in range(1, 4):
         send(True, lambda d=d: copy(d_all.at[r], d_all.at[r], db_s.at[d], db_r.at[k], (along_x(d), c)))
+    send(True, lambda: copy(c_all.at[c], c_all.at[c], ca_s.at[0], ca_r.at[c], (r, far)))
     send(True, lambda: copy(d_all.at[r], d_all.at[r], dc_s.at[0], dc_r.at[k], sib))
+    first_half, second_half = pl.ds(0, NC // 2), pl.ds(NC // 2, NC // 2)
+    arrived(d_all.at[near], db_r.at[near // 2])
+    for d in range(1, 4):
+        part = d_all.at[near, first_half]
+        send(True, lambda d=d, part=part: copy(part, part, db_s.at[3 + d], dh_r.at[0, near // 2], (along_x(d), c)))
+    send(True, lambda: copy(d_all.at[near], d_all.at[near], dc_s.at[1], dc_r.at[near // 2], sib))
     arrived(c_all.at[far], ca_r.at[far])
     for d in range(1, 4):
         send(True, lambda d=d: copy(c_all.at[far], c_all.at[far], ca_s.at[3 + d], ca_r.at[far], (r, along_y(d))))
-    arrived(d_all.at[near], db_r.at[near // 2])
-    for d in range(1, 4):
-        send(True, lambda d=d: copy(d_all.at[near], d_all.at[near], db_s.at[3 + d], db_r.at[near // 2], (along_x(d), c)))
-    send(True, lambda: copy(d_all.at[near], d_all.at[near], dc_s.at[1], dc_r.at[near // 2], sib))
-    for h in range(2):
-        for d in range(1, 4):
-            of = (along_x(d) + 8 * h) % NA
-            arrived(d_all.at[of], db_r.at[of // 2])
-            send(True, lambda d=d, h=h, of=of: copy(d_all.at[of], d_all.at[of], dc_s.at[1 + 3 * h + d], dc_r.at[of // 2], sib))
+    for d in range(1, 4):
+        of = along_x(d)
+        arrived(d_all.at[of], db_r.at[of // 2])
+        part = d_all.at[of, second_half]
+        send(True, lambda d=d, of=of, part=part: copy(part, part, dh_s.at[d], dh_r.at[1, of // 2], (near, c)))
+        send(True, lambda d=d, of=of: copy(d_all.at[of], d_all.at[of], dc_s.at[1 + d], dc_r.at[of // 2], sib))
+    for d in range(1, 4):
+        of = (along_x(d) + 8) % NA
+        arrived(d_all.at[of, first_half], dh_r.at[0, of // 2])
+        arrived(d_all.at[of, second_half], dh_r.at[1, of // 2])
+        send(True, lambda d=d, of=of: copy(d_all.at[of], d_all.at[of], dc_s.at[4 + d], dc_r.at[of // 2], sib))
     for d in range(1, 4):
         for of in (along_y(d), (along_y(d) + 4) % NC):
             arrived(c_all.at[of], ca_r.at[of])
@@ -403,9 +417,9 @@
             pltpu.VMEM((2, NS, B, W), F32),
             pltpu.VMEM((2, NS, B, W), F32),
             pltpu.VMEM((NS, B, W), F32),
+            pltpu.VMEM((NS, 4, B, LANES), F32),
             pltpu.VMEM((4, NS, B, LANES), F32),
-            pltpu.VMEM((4, NS, B, LANES), F32),
-            pltpu.VMEM((4, NS, B, LANES), F32),
+            pltpu.VMEM((NS, 4, B, LANES), F32),
             pltpu.VMEM((4, NS, B, LANES), F32),
             pltpu.VMEM((NS, B, LANES), F32),
             pltpu.VMEM((NS, B, LANES), F32),
@@ -413,16 +427,17 @@
             pltpu.VMEM((2, B, LANES), F32),
             pltpu.VMEM((NA, PIECE, LANES), F32),
             pltpu.VMEM((NA, PIECE, LANES), F32),
-            dma((64,)), dma((4,)),
-            dma((2,)), dma((2,)),
+            dma((40,)), dma((4,)),
+            dma((3,)), dma((3,)),
             dma((1,)), dma((1,)),
-            dma((4,)), dma((4,)), dma((4,)), dma((4,)),
+            dma((NS, 4)), dma((4,)), dma((NS, 4)), dma((4,)),
             dma((1,)), dma((1,)),
             dma((2,)), dma((2,)),
             dma((NC,)), dma((NC,)),
             dma((NA,)), dma((NA,)),
             dma((NC,)), dma((NC,)),
             dma((NC,)), dma((NC,)),
+            dma((4,)), dma((2, NC)),
             dma((NC,)), dma((NC,)),
         ],
         compiler_params=pltpu.CompilerParams(has_side_effects=True, collective_id=0),

time: 89.9 us -> 82.5 us (0.918)
  Pallas kernels: 89.1 us -> 81.7 us
    pallas_call x1, Pallas kernels: 85.6 us -> 78.2 us  [shards(): pl.pallas_call(exchange, out_shape=(pltpu.VMEM((NC, B, LANES), F32), pltp...]
where the time goes in v4:
time: 82.5 us; the launch traced here: 82.4 us
  Pallas kernels  81.7 us (99%)
    pallas_call x1, Pallas kernels, shards(): pl.pallas_call(exchange, out_shape=(pltpu.VMEM((NC, B, LANES), F32), pltp...  78.2 us
    pallas_call x1, Pallas kernels, shards(): pl.pallas_call(place, out_shape=(jax.ShapeDtypeStruct((4 * B, NS * W), F3...  3.52 us

profile of v4, /device:TPU:1, one launch (start us, length us, event | category | flops | bytes accessed | tf_op | source)
XLA Modules:
  0.0 82.4 jit_solution(205801441653388848)
XLA Ops:
  0.6 78.2 %exchange.1 = (f32[8,256,128]{2,1,0:T(8,128)S(1)}, f32[16,8,32,128]{3,2,1,0:T(8,128)S(1)}) custom-call(s32[2,16]{1,0:T(2,128)} %tile_list.3, s32[2,16]{1,0:T(2,128)} %tile_valid.3, f32[1024,2048]{1,0:T(8,128)} %front_hbm.1, f32[256,1024]{1,0:T(8,128)} %factor_hbm.1, f32[2,512,512]{2,1,0:T(8,128)} %lower_hbm.1, f32[2,512]{1,0:T(2,128)} %pivot_hbm.1), custom_call_target="tpu_custom_call" | custom-call | tf_op jit(solution)/shard_map/exchange/pallas_call | solution.py:400
  78.8 3.5 %place.1 = (f32[1024,1024]{1,0:T(8,128)}, f32[2,512,512]{2,1,0:T(8,128)}) custom-call(s32[2,16]{1,0:T(2,128)} %tile_list.3, s32[2,16]{1,0:T(2,128)} %tile_valid.3, f32[8,256,128]{2,1,0:T(8,128)S(1)} %get-tuple-element.4.c_all, f32[16,8,32,128]{3,2,1,0:T(8,128)S(1)} %get-tuple-element.5.d_all), custom_call_target="tpu_custom_call" | custom-call | tf_op jit(solution)/shard_map/place/pallas_call | solution.py:447

commit v5 on v4

--- a/solution.py
+++ b/solution.py
@@ -90,18 +90,12 @@
 
     fetch = [
         pltpu.make_async_copy(factor_hbm, factor, in_s.at[0]),
-        pltpu.make_async_copy(lower_hbm, lower_v, in_s.at[1]),
-        pltpu.make_async_copy(pivot_hbm, pivot, in_s.at[2]),
+        pltpu.make_async_copy(lower_hbm.at[0], lower_v.at[0], in_s.at[1]),
+        pltpu.make_async_copy(lower_hbm.at[1], lower_v.at[1], in_s.at[2]),
+        pltpu.make_async_copy(pivot_hbm, pivot, in_s.at[4]),
     ]
     for item in fetch:
         item.start()
-
-    @pl.when(lower | diag)
-    def _():
-        for i in range(4):
-            for j in range(8):
-                part = front_hbm.at[i * B : (i + 1) * B, j * B : (j + 1) * B]
-                pltpu.make_async_copy(part, front.at[i, j], in_s.at[3]).start()
 
     entry = pltpu.get_barrier_semaphore()
 
@@ -118,12 +112,14 @@
 
     i0 = lax.broadcasted_iota(jnp.int32, (W, W), 0)
     i1 = lax.broadcasted_iota(jnp.int32, (W, W), 1)
-    fetch[0].wait()
-    fetch[1].wait()
-    for s in range(NS):
+    def normalize(s):
+        fetch[1 + s].wait()
         inv = jnp.where(i0 > i1, lower_v[s], jnp.where(i0 == i1, 1.0, 0.0))
         keep = (tile_valid[s, r] > 0).astype(F32)
         norm[s] = mm(split(factor[:, s * W : (s + 1) * W] * keep), split(inv))
+
+    fetch[0].wait()
+    normalize(0)
     pl.semaphore_wait(entry, jnp.where(diag, 36, 38))
 
     def give(cond, s, part, sem, arrival, row, col):
@@ -131,6 +127,8 @@
 
     count = 0
     for s in range(NS):
+        if s == 1:
+            normalize(1)
         for j in (2 * s, 2 * s + 1):
             for d in range(4):
                 alpha, side = FULL[d][j]
@@ -147,6 +145,13 @@
 
     @pl.when(lower | diag)
     def _():
+        for i in range(4):
+            for j in range(8):
+                part = front_hbm.at[i * B : (i + 1) * B, j * B : (j + 1) * B]
+                pltpu.make_async_copy(part, front.at[i, j], in_s.at[3]).start()
+
+    @pl.when(lower | diag)
+    def _():
         pltpu.make_async_copy(front, front, in_s.at[3]).wait()
         b0 = lax.broadcasted_iota(jnp.int32, (B, B), 0)
         b1 = lax.broadcasted_iota(jnp.int32, (B, B), 1)
@@ -186,10 +191,11 @@
                 q_out[d, s] = q_loc[q, s, :, lanes] + q_rx[s, :, lanes]
         cq_rx[x] = q_out[x]
 
-    for d in range(4):
-        send(lower & (x != d), lambda d=d: copy(q_out.at[d], cq_rx.at[x], q_ss.at[d], cq_r.at[x], (8 * zl + 2 * d + q, c)))
-
-    fetch[2].wait()
+    for i in (2, 1, 3):
+        d = (x + i) % 4
+        send(lower, lambda i=i, d=d: copy(q_out.at[d], cq_rx.at[x], q_ss.at[i], cq_r.at[x], (8 * zl + 2 * d + q, c)))
+
+    fetch[3].wait()
     for s in range(NS):
 
         @pl.when(zh == s)
@@ -234,10 +240,11 @@
         def _():
             put(mm(split(tiles[2 * s]), split(norm[s])) + q_rx[s])
 
-        for d in range(4):
+        for i in (2, 1, 3):
+            d = (y + i) % 4
             send(
-                (lower | diag) & (y != d),
-                lambda s=s, d=d: copy(p_out.at[s, d], cp_rx.at[s, y], p_ss.at[s, d], cp_r.at[s, y], (r, 4 * zh + d)),
+                lower | diag,
+                lambda s=s, i=i, d=d: copy(p_out.at[s, d], cp_rx.at[s, y], p_ss.at[s, i], cp_r.at[s, y], (r, 4 * zh + d)),
             )
 
     def gather(out, parts, sems, has, here):
@@ -308,8 +315,6 @@
     def along_x(d):
         return r - r % 8 + (r + 2 * d) % 8
 
-    for d in range(1, 4):
-        send(True, lambda d=d: copy(c_all.at[c], c_all.at[c], ca_s.at[d], ca_r.at[c], (r, along_y(d))))
     acc = base[pl.ds(pl.multiple_of(r * PIECE, PIECE), PIECE), :] - d_part[r]
     for d in range(1, NA):
         of = (r + d) % NA
@@ -325,18 +330,20 @@
         arrived(d_all.at[r, of], da_r.at[of])
     near = (r + 8) % NA
     send(True, lambda: copy(d_all.at[r], d_all.at[r], db_s.at[0], db_r.at[k], (near, c)))
-    for d in range(1, 4):
+    for d in (2, 1, 3):
         send(True, lambda d=d: copy(d_all.at[r], d_all.at[r], db_s.at[d], db_r.at[k], (along_x(d), c)))
+    for d in (2, 1, 3):
+        send(True, lambda d=d: copy(c_all.at[c], c_all.at[c], ca_s.at[d], ca_r.at[c], (r, along_y(d))))
     send(True, lambda: copy(c_all.at[c], c_all.at[c], ca_s.at[0], ca_r.at[c], (r, far)))
     send(True, lambda: copy(d_all.at[r], d_all.at[r], dc_s.at[0], dc_r.at[k], sib))
     first_half, second_half = pl.ds(0, NC // 2), pl.ds(NC // 2, NC // 2)
     arrived(d_all.at[near], db_r.at[near // 2])
-    for d in range(1, 4):
+    for d in (2, 1, 3):
         part = d_all.at[near, first_half]
         send(True, lambda d=d, part=part: copy(part, part, db_s.at[3 + d], dh_r.at[0, near // 2], (along_x(d), c)))
     send(True, lambda: copy(d_all.at[near], d_all.at[near], dc_s.at[1], dc_r.at[near // 2], sib))
     arrived(c_all.at[far], ca_r.at[far])
-    for d in range(1, 4):
+    for d in (2, 1, 3):
         send(True, lambda d=d: copy(c_all.at[far], c_all.at[far], ca_s.at[3 + d], ca_r.at[far], (r, along_y(d))))
     for d in range(1, 4):
         of = along_x(d)
@@ -413,7 +420,7 @@
             pltpu.VMEM((2 * NS, B, B), F32),
             pltpu.VMEM((NS, B, W), F32),
             pltpu.VMEM((W, LANES), F32),
-            dma((4,)),
+            dma((5,)),
             pltpu.VMEM((2, NS, B, W), F32),
             pltpu.VMEM((2, NS, B, W), F32),
             pltpu.VMEM((NS, B, W), F32),

time: 82.5 us -> 80.8 us (0.979)
  Pallas kernels: 81.7 us -> 79.9 us
    pallas_call x1, Pallas kernels: 78.2 us -> 76.3 us  [shards(): pl.pallas_call(exchange, out_shape=(pltpu.VMEM((NC, B, LANES), F32), pltp...]
where the time goes in v5:
time: 80.8 us; the launch traced here: 80.5 us
  Pallas kernels  79.9 us (99%)
    pallas_call x1, Pallas kernels, shards(): pl.pallas_call(exchange, out_shape=(pltpu.VMEM((NC, B, LANES), F32), pltp...  76.3 us
    pallas_call x1, Pallas kernels, shards(): pl.pallas_call(place, out_shape=(jax.ShapeDtypeStruct((4 * B, NS * W), F3...  3.52 us

profile of v5, /device:TPU:1, one launch (start us, length us, event | category | flops | bytes accessed | tf_op | source)
XLA Modules:
  0.0 80.5 jit_solution(5790164740334956249)
XLA Ops:
  0.6 76.3 %exchange.1 = (f32[8,256,128]{2,1,0:T(8,128)S(1)}, f32[16,8,32,128]{3,2,1,0:T(8,128)S(1)}) custom-call(s32[2,16]{1,0:T(2,128)} %tile_list.3, s32[2,16]{1,0:T(2,128)} %tile_valid.3, f32[1024,2048]{1,0:T(8,128)} %front_hbm.1, f32[256,1024]{1,0:T(8,128)} %factor_hbm.1, f32[2,512,512]{2,1,0:T(8,128)} %lower_hbm.1, f32[2,512]{1,0:T(2,128)} %pivot_hbm.1), custom_call_target="tpu_custom_call" | custom-call | tf_op jit(solution)/shard_map/exchange/pallas_call | solution.py:407
  77.0 3.5 %place.1 = (f32[1024,1024]{1,0:T(8,128)}, f32[2,512,512]{2,1,0:T(8,128)}) custom-call(s32[2,16]{1,0:T(2,128)} %tile_list.3, s32[2,16]{1,0:T(2,128)} %tile_valid.3, f32[8,256,128]{2,1,0:T(8,128)S(1)} %get-tuple-element.4.c_all, f32[16,8,32,128]{3,2,1,0:T(8,128)S(1)} %get-tuple-element.5.d_all), custom_call_target="tpu_custom_call" | custom-call | tf_op jit(solution)/shard_map/place/pallas_call | solution.py:454
